TPU v7x, 32 devices: a whole 2x2x4 slice. The times are simulated.
32 devices in a mesh: tensor: 4 (over z), context: 4 (over y, core), dp: 2 (over x).
Axes of the slice: x: 2, y: 2, z: 4, core: 2. Of those that a mesh axis runs over, the one named last changes fastest.
Arguments:
- inputs: bfloat16 [2, 3072, 768], P('dp', ('context', 'tensor')), may hold values from -6 to 6
- first_gain: float32 [768], replicated, may hold values from 0.5 to 1.5
- first_shift: float32 [768], replicated, may hold values from -1 to 1
- project_weight: bfloat16 [3, 768, 768], P(None, None, 'tensor'), may hold values from -0.21875 to 0.21875
- project_bias: float32 [2, 768], P(None, 'tensor'), may hold values from -1.5 to 1.5
- attend_weight: bfloat16 [768, 768], P('tensor'), may hold values from -1.25 to 1.25
- attend_bias: float32 [768], replicated, may hold values from -1.5 to 1.5
- second_gain: float32 [768], replicated, may hold values from 0.5 to 1.5
- second_shift: float32 [768], replicated, may hold values from -1 to 1
- expand_weight: bfloat16 [768, 3072], P(None, 'tensor'), may hold values from -0.21875 to 0.21875
- expand_bias: float32 [3072], P('tensor'), may hold values from -1.5 to 1.5
- shrink_weight: bfloat16 [3072, 768], P('tensor'), may hold values from -0.109375 to 0.109375
- shrink_bias: float32 [768], replicated, may hold values from -1.5 to 1.5
- segments: int32 [2, 3072], P('dp'), may hold values from 0 to 15, never falling along the last dimension, each value on 1 to 1536 neighbouring positions
- block_order: int32 [8], replicated, may hold values from 0 to 7, each once
- cotangent: bfloat16 [2, 3072, 768], P('dp', ('context', 'tensor')), may hold values from -6 to 6
Outputs:
- outputs: bfloat16 [2, 3072, 768], P('dp', ('context', 'tensor'))
- grad_inputs: bfloat16 [2, 3072, 768], P('dp', ('context', 'tensor'))
- grad_first_gain: float32 [768], replicated
- grad_first_shift: float32 [768], replicated
- grad_project_weight: float32 [3, 768, 768], P(None, None, 'tensor')
- grad_project_bias: float32 [2, 768], P(None, 'tensor')
- grad_attend_weight: float32 [768, 768], P('tensor')
- grad_attend_bias: float32 [768], replicated
- grad_second_gain: float32 [768], replicated
- grad_second_shift: float32 [768], replicated
- grad_expand_weight: float32 [768, 3072], P(None, 'tensor')
- grad_expand_bias: float32 [3072], P('tensor')
- grad_shrink_weight: float32 [3072, 768], P('tensor')
- grad_shrink_bias: float32 [768], replicated
Inputs may be any that keep to these rules, and one draw needn't show every extreme that they name: `segments`: in each sequence the document numbers never fall; every number appears, each document has 1 to 1536 tokens and one has exactly 1536. Each value appears once: stored block b of 384 tokens holds natural block block_order[b].
All inputs are finite; a program needn't handle non-finite values.
Results may differ from a plain program's by a relative error of at most 0.02.
Values may be sent and summed in bfloat16 or wider, within the bound.
A program may use at most 128 MiB of HBM per device.

v0:
```python
import functools

import jax
import jax.numpy as jnp
from jax import lax
from jax.experimental import pallas as pl
from jax.experimental.pallas import tpu as pltpu
from jax.sharding import PartitionSpec as P

HEAD_DIM = 64
NEG_FILL = -1e30
NORM_EPS = 1e-05
DOC_LIMIT = 16
MESH = pl.DeviceIdType.MESH
VM = pl.BlockSpec(memory_space=pltpu.VMEM)
SM = pl.BlockSpec(memory_space=pltpu.SMEM)
DMA = pltpu.SemaphoreType.DMA


def remote_params(collective_id, mib=16):
    return pltpu.CompilerParams(
        collective_id=collective_id, has_side_effects=True, vmem_limit_bytes=mib << 20
    )


HB = pl.BlockSpec(memory_space=pltpu.HBM)


def copies(pairs, sems):
    return [pltpu.make_async_copy(src, dst, sems.at[at]) for at, (src, dst) in enumerate(pairs)]


def row(ref):
    return ref[...].reshape(1, -1)


def line_barrier(me, n):
    bar = pltpu.get_barrier_semaphore()

    @pl.when(me > 0)
    def _():
        pl.semaphore_signal(bar, inc=1, device_id={"tensor": me - 1}, device_id_type=MESH)

    @pl.when(me < n - 1)
    def _():
        pl.semaphore_signal(bar, inc=1, device_id={"tensor": me + 1}, device_id_type=MESH)

    pl.semaphore_wait(bar, jnp.where(me > 0, 1, 0) + jnp.where(me < n - 1, 1, 0))


def gather_kernel(n, x_ref, o_ref, send, recv, loc):
    me = lax.axis_index("tensor")
    line_barrier(me, n)
    own = pltpu.make_async_copy(x_ref, o_ref.at[me], loc)
    own.start()

    def copy(d, s):
        shard = jnp.clip(me - s if d == 0 else me + s, 0, n - 1)
        return pltpu.make_async_remote_copy(
            src_ref=x_ref if s == 0 else o_ref.at[shard],
            dst_ref=o_ref.at[shard],
            send_sem=send.at[d, s],
            recv_sem=recv.at[d, s],
            device_id={"tensor": jnp.clip(me + 1 if d == 0 else me - 1, 0, n - 1)},
            device_id_type=MESH,
        )

    def sends(d, s):
        return (me - s >= 0) & (me < n - 1) if d == 0 else (me + s < n) & (me > 0)

    def gets(d, s):
        return me - 1 - s >= 0 if d == 0 else me + 1 + s < n

    def landed(d, s):
        shard = jnp.clip(me - 1 - s if d == 0 else me + 1 + s, 0, n - 1)
        return pltpu.make_async_copy(o_ref.at[shard], o_ref.at[shard], recv.at[d, s])

    for s in range(n - 1):
        for d in range(2):
            if s > 0:

                @pl.when(gets(d, s - 1))
                def _():
                    landed(d, s - 1).wait()

            @pl.when(sends(d, s))
            def _():
                copy(d, s).start()

    for d in range(2):

        @pl.when(gets(d, n - 2))
        def _():
            landed(d, n - 2).wait()

        for s in range(n - 1):

            @pl.when(sends(d, s))
            def _():
                copy(d, s).wait_send()

    own.wait()


def gather_rows(x, n, collective_id):
    rows, cols = x.shape
    return pl.pallas_call(
        functools.partial(gather_kernel, n),
        out_shape=jax.ShapeDtypeStruct((n, rows, cols), x.dtype),
        in_specs=[VM],
        out_specs=VM,
        scratch_shapes=[DMA((2, n - 1)), DMA((2, n - 1)), DMA],
        compiler_params=remote_params(collective_id),
    )(x).reshape(n * rows, cols)


def scatter_kernel(n, x_ref, o_ref, buf, tmp, send, recv):
    me = lax.axis_index("tensor")
    line_barrier(me, n)

    def term(d, k):
        return n - 1 - k if d == 0 else k

    def sends(d, k):
        return me < n - 1 - k if d == 0 else me > k

    def behind(d):
        return me > 0 if d == 0 else me < n - 1

    def copy(d, k, first):
        return pltpu.make_async_remote_copy(
            src_ref=x_ref.at[term(d, k)] if first else tmp.at[d, k],
            dst_ref=buf.at[d, k],
            send_sem=send.at[d, k],
            recv_sem=recv.at[d, k],
            device_id={"tensor": jnp.clip(me + 1 if d == 0 else me - 1, 0, n - 1)},
            device_id_type=MESH,
        )

    def landed(d, k):
        return pltpu.make_async_copy(buf.at[d, k], buf.at[d, k], recv.at[d, k])

    for d in range(2):

        @pl.when(jnp.logical_not(behind(d)))
        def _():
            for k in range(n - 1):
                copy(d, k, True).start()

    for k in range(n - 1):
        for d in range(2):

            @pl.when(behind(d) & sends(d, k))
            def _():
                landed(d, k).wait()
                both = buf[d, k].astype(jnp.float32) + x_ref[term(d, k)].astype(jnp.float32)
                tmp[d, k] = both.astype(tmp.dtype)
                copy(d, k, False).start()

    o_ref[...] = x_ref[me].astype(jnp.float32)
    for d in range(2):
        for k in range(n - 1):

            @pl.when(behind(d) & (me == term(d, k)))
            def _():
                landed(d, k).wait()
                o_ref[...] += buf[d, k].astype(jnp.float32)

    for d in range(2):
        for k in range(n - 1):

            @pl.when(sends(d, k))
            def _():
                copy(d, k, False).wait_send()


def scatter_rows(x, n, collective_id):
    rows, cols = x.shape
    own = rows // n
    return pl.pallas_call(
        functools.partial(scatter_kernel, n),
        out_shape=jax.ShapeDtypeStruct((own, cols), jnp.float32),
        in_specs=[VM],
        out_specs=VM,
        scratch_shapes=[
            pltpu.VMEM((2, n - 1, own, cols), x.dtype),
            pltpu.VMEM((2, n - 1, own, cols), x.dtype),
            DMA((2, n - 1)),
            DMA((2, n - 1)),
        ],
        compiler_params=remote_params(collective_id),
    )(x.reshape(n, own, cols))


def group_barrier(axes, sizes):
    mine = [lax.axis_index(name) for name in axes]
    place = sum_index(mine, sizes)
    total = 1
    for size in sizes:
        total *= size
    bar = pltpu.get_barrier_semaphore()
    for shift in range(1, total):
        other = lax.rem(place + shift, total)
        pl.semaphore_signal(bar, inc=1, device_id=spread(other, axes, sizes), device_id_type=MESH)
    pl.semaphore_wait(bar, total - 1)
    return place, total


def sum_index(mine, sizes):
    place = 0
    for at, size in zip(mine, sizes):
        place = place * size + at
    return place


def spread(place, axes, sizes):
    found = {}
    for name, size in reversed(tuple(zip(axes, sizes))):
        found[name] = lax.rem(place, size)
        place = lax.div(place, size)
    return found


def to_heads_kernel(nc, heads, x_ref, o_ref, send, recv, loc):
    me, _ = group_barrier(("context",), (nc,))

    def copy(shift):
        other = lax.rem(me + shift, nc)
        return other, pltpu.make_async_remote_copy(
            src_ref=x_ref.at[:, jnp.minimum(other, heads - 1)],
            dst_ref=o_ref.at[me],
            send_sem=send.at[shift],
            recv_sem=recv.at[shift],
            device_id={"context": other},
            device_id_type=MESH,
        )

    for shift in range(1, nc):
        other, item = copy(shift)

        @pl.when(other < heads)
        def _():
            item.start()

    own = pltpu.make_async_copy(x_ref.at[:, jnp.minimum(me, heads - 1)], o_ref.at[me], loc)
    own.start()
    own.wait()

    @pl.when(me < heads)
    def _():
        for shift in range(1, nc):
            source = lax.rem(me + nc - shift, nc)
            pltpu.make_async_copy(o_ref.at[source], o_ref.at[source], recv.at[shift]).wait()

    for shift in range(1, nc):
        other, item = copy(shift)

        @pl.when(other < heads)
        def _():
            item.wait_send()


def to_heads(x, nc, collective_id):
    heads = x.shape[1]
    return pl.pallas_call(
        functools.partial(to_heads_kernel, nc, heads),
        out_shape=jax.ShapeDtypeStruct((nc, x.shape[0]) + x.shape[2:], x.dtype),
        in_specs=[VM],
        out_specs=VM,
        scratch_shapes=[DMA((nc,)), DMA((nc,)), DMA],
        compiler_params=remote_params(collective_id),
    )(x)


def from_heads_kernel(nc, heads, x_ref, o_ref, send, recv, loc):
    me, _ = group_barrier(("context",), (nc,))

    def copy(shift):
        other = lax.rem(me + shift, nc)
        return pltpu.make_async_remote_copy(
            src_ref=x_ref.at[other],
            dst_ref=o_ref.at[:, jnp.minimum(me, heads - 1)],
            send_sem=send.at[shift],
            recv_sem=recv.at[shift],
            device_id={"context": other},
            device_id_type=MESH,
        )

    @pl.when(me < heads)
    def _():
        for shift in range(1, nc):
            copy(shift).start()
        own = pltpu.make_async_copy(x_ref.at[me], o_ref.at[:, me], loc)
        own.start()
        own.wait()

    for shift in range(1, nc):
        source = lax.rem(me + nc - shift, nc)

        @pl.when(source < heads)
        def _():
            at = jnp.minimum(source, heads - 1)
            pltpu.make_async_copy(o_ref.at[:, at], o_ref.at[:, at], recv.at[shift]).wait()

    @pl.when(me < heads)
    def _():
        for shift in range(1, nc):
            copy(shift).wait_send()


def from_heads(x, nc, heads, collective_id):
    return pl.pallas_call(
        functools.partial(from_heads_kernel, nc, heads),
        out_shape=jax.ShapeDtypeStruct((x.shape[1], heads) + x.shape[2:], x.dtype),
        in_specs=[VM],
        out_specs=VM,
        scratch_shapes=[DMA((nc,)), DMA((nc,)), DMA],
        compiler_params=remote_params(collective_id),
    )(x)


AXES = ("context", "tensor")


def rows_kernel(nc, nt, heads, x_ref, o_ref, send, recv, loc):
    me, total = group_barrier(AXES, (nc, nt))
    my_ctx, my_ten = lax.axis_index("context"), lax.axis_index("tensor")
    my_head = my_ten * heads + jnp.minimum(my_ctx, heads - 1)

    def copy(shift):
        other = lax.rem(me + shift, total)
        return pltpu.make_async_remote_copy(
            src_ref=x_ref.at[other],
            dst_ref=o_ref.at[my_head],
            send_sem=send.at[shift],
            recv_sem=recv.at[shift],
            device_id=spread(other, AXES, (nc, nt)),
            device_id_type=MESH,
        )

    @pl.when(my_ctx < heads)
    def _():
        for shift in range(1, total):
            copy(shift).start()
        own = pltpu.make_async_copy(x_ref.at[me], o_ref.at[my_head], loc)
        own.start()
        own.wait()

    for shift in range(1, total):
        source = lax.rem(me + total - shift, total)
        ctx, ten = lax.div(source, nt), lax.rem(source, nt)

        @pl.when(ctx < heads)
        def _():
            at = ten * heads + jnp.minimum(ctx, heads - 1)
            pltpu.make_async_copy(o_ref.at[at], o_ref.at[at], recv.at[shift]).wait()

    @pl.when(my_ctx < heads)
    def _():
        for shift in range(1, total):
            copy(shift).wait_send()


def to_rows(x, nc, nt, heads, collective_id):
    total = nc * nt
    return pl.pallas_call(
        functools.partial(rows_kernel, nc, nt, heads),
        out_shape=jax.ShapeDtypeStruct((nt * heads,) + x.shape[1:], x.dtype),
        in_specs=[VM],
        out_specs=VM,
        scratch_shapes=[DMA((total,)), DMA((total,)), DMA],
        compiler_params=remote_params(collective_id),
    )(x)


def rows_back_kernel(nc, nt, heads, x_ref, o_ref, send, recv, loc):
    me, total = group_barrier(AXES, (nc, nt))
    my_ctx, my_ten = lax.axis_index("context"), lax.axis_index("tensor")

    def copy(shift):
        other = lax.rem(me + shift, total)
        ctx, ten = lax.div(other, nt), lax.rem(other, nt)
        return ctx < heads, pltpu.make_async_remote_copy(
            src_ref=x_ref.at[ten * heads + jnp.minimum(ctx, heads - 1)],
            dst_ref=o_ref.at[me],
            send_sem=send.at[shift],
            recv_sem=recv.at[shift],
            device_id={"context": ctx, "tensor": ten},
            device_id_type=MESH,
        )

    for shift in range(1, total):
        goes, item = copy(shift)

        @pl.when(goes)
        def _():
            item.start()

    own = pltpu.make_async_copy(
        x_ref.at[my_ten * heads + jnp.minimum(my_ctx, heads - 1)], o_ref.at[me], loc
    )
    own.start()
    own.wait()

    @pl.when(my_ctx < heads)
    def _():
        for shift in range(1, total):
            source = lax.rem(me + total - shift, total)
            pltpu.make_async_copy(o_ref.at[source], o_ref.at[source], recv.at[shift]).wait()

    for shift in range(1, total):
        goes, item = copy(shift)

        @pl.when(goes)
        def _():
            item.wait_send()


def rows_back(x, nc, nt, heads, collective_id):
    total = nc * nt
    return pl.pallas_call(
        functools.partial(rows_back_kernel, nc, nt, heads),
        out_shape=jax.ShapeDtypeStruct((total,) + x.shape[1:], x.dtype),
        in_specs=[VM],
        out_specs=VM,
        scratch_shapes=[DMA((total,)), DMA((total,)), DMA],
        compiler_params=remote_params(collective_id),
    )(x)


def vectors_kernel(names, sizes, shared, x_ref, o_ref, now, *rest):
    bufs, sems = rest[: len(names)], rest[len(names) :]
    bar = pltpu.get_barrier_semaphore()
    for name, size in zip(names, sizes):
        me = lax.axis_index(name)
        for shift in range(1, size):
            pl.semaphore_signal(
                bar, inc=1, device_id={name: lax.rem(me + shift, size)}, device_id_type=MESH
            )
    pl.semaphore_wait(bar, sum(sizes) - len(sizes))
    for stage, (name, size) in enumerate(zip(names, sizes)):
        buf, send, recv = bufs[stage], sems[2 * stage], sems[2 * stage + 1]
        me = lax.axis_index(name)

        def copy(shift):
            return pltpu.make_async_remote_copy(
                src_ref=now.at[stage] if stage else x_ref.at[0],
                dst_ref=buf.at[me],
                send_sem=send.at[shift],
                recv_sem=recv.at[shift],
                device_id={name: lax.rem(me + shift, size)},
                device_id_type=MESH,
            )

        for shift in range(1, size):
            copy(shift).start()
        buf[me] = now[stage] if stage else x_ref[0]
        for shift in range(1, size):
            source = lax.rem(me + size - shift, size)
            pltpu.make_async_copy(buf.at[source], buf.at[source], recv.at[shift]).wait()
        total = buf[0]
        for at in range(1, size):
            total = total + buf[at]
        if stage == 0:
            row = lax.broadcasted_iota(jnp.int32, total.shape, 0)
            total = jnp.where(row < shared, total, x_ref[0])
        if stage + 1 < len(names):
            now[stage + 1] = total
        else:
            o_ref[...] = total
        for shift in range(1, size):
            copy(shift).wait_send()


def sum_vectors(rows, shared, mesh_sizes, collective_id):
    names = ("tensor", "context", "dp")
    sizes = tuple(mesh_sizes[name] for name in names)
    shape = rows.shape
    return pl.pallas_call(
        functools.partial(vectors_kernel, names, sizes, shared),
        out_shape=jax.ShapeDtypeStruct(shape, jnp.float32),
        in_specs=[VM],
        out_specs=VM,
        scratch_shapes=[pltpu.VMEM((len(names),) + shape, jnp.float32)]
        + [pltpu.VMEM((size,) + shape, jnp.float32) for size in sizes]
        + [DMA((size,)) for size in sizes for _ in range(2)],
        compiler_params=remote_params(collective_id),
    )(rows[None])


class PlaneSum:
    def __init__(self, u, p, o, bufs=None, spread=None):
        self.u, self.p, self.o = u, p, o
        if bufs is not None:
            self.rc, self.s1, self.ra, self.rb, self.sa, self.sb, self.ta, self.tb = bufs[:8]
            self.send1, self.recv1 = bufs[8:]
        if spread is not None:
            self.send2, self.recv2, self.loc = spread
        ctx, self.x = lax.axis_index("context"), lax.axis_index("dp")
        self.core, self.y = lax.rem(ctx, 2), lax.div(ctx, 2)
        self.chip_peer = {"context": ctx + 1 - 2 * self.core}
        self.y_peer = {"context": lax.rem(ctx + 2, 4)}
        self.x_peer = {"dp": 1 - self.x}

    @staticmethod
    def reduce_scratch(shape, dtype):
        tail = tuple(shape[1:])
        bufs = [pltpu.VMEM((count,) + tail, dtype) for count in (8, 8, 2, 2, 2, 2, 1, 1)]
        return bufs + [DMA((5,)), DMA((5,))]

    @staticmethod
    def spread_scratch():
        return [DMA((5,)), DMA((5,)), DMA((2,))]

    @staticmethod
    def greet(bar):
        ctx, x = lax.axis_index("context"), lax.axis_index("dp")
        for peer in (
            {"context": ctx + 1 - 2 * lax.rem(ctx, 2)},
            {"context": lax.rem(ctx + 2, 4)},
            {"dp": 1 - x},
        ):
            pl.semaphore_signal(bar, inc=1, device_id=peer, device_id_type=MESH)
        return 3

    def copy(self, at, src, dst, peer):
        send, recv = (self.send1, self.recv1) if at < 5 else (self.send2, self.recv2)
        return pltpu.make_async_remote_copy(
            src_ref=src,
            dst_ref=dst,
            send_sem=send.at[at % 5],
            recv_sem=recv.at[at % 5],
            device_id=peer,
            device_id_type=MESH,
        )

    def got(self, at, ref):
        recv = self.recv1 if at < 5 else self.recv2
        pltpu.make_async_copy(ref, ref, recv.at[at % 5]).wait()

    def add(self, out, left, right):
        f32 = jnp.float32
        out[...] = (left[...].astype(f32) + right[...].astype(f32)).astype(out.dtype)

    def mine(self, half):
        if half == 0:
            return pl.ds(self.core * 8 + 2 * self.x + self.y, 1)
        return pl.ds(self.core * 8 + 4 + 2 * self.y + self.x, 1)

    def hop(self, at):
        x, y, core = self.x, self.y, self.core
        o, p = self.o, self.p
        pair_a, pair_b = pl.ds(core * 8 + 2 * x, 2), pl.ds(core * 8 + 4 + 2 * y, 2)
        one = lambda at: pl.ds(at, 1)
        return [
            lambda: self.copy(0, self.by_core(1 - core), self.rc, self.chip_peer),
            lambda: self.copy(1, self.quarter(0, 1 - x), self.ra, self.x_peer),
            lambda: self.copy(2, self.quarter(1, 1 - y), self.rb, self.y_peer),
            lambda: self.copy(3, self.eighth(0, 1 - y), self.ta, self.y_peer),
            lambda: self.copy(4, self.eighth(1, 1 - x), self.tb, self.x_peer),
            lambda: self.copy(5, p.at[one(0)], o.at[self.mine(0)], self.y_peer),
            lambda: self.copy(6, p.at[one(1)], o.at[self.mine(1)], self.x_peer),
            lambda: self.copy(7, o.at[pair_a], o.at[pair_a], self.x_peer),
            lambda: self.copy(8, o.at[pair_b], o.at[pair_b], self.y_peer),
            lambda: self.copy(9, o.at[pl.ds(core * 8, 8)], o.at[pl.ds(core * 8, 8)], self.chip_peer),
        ][at]()

    def begin(self):
        self.hop(0).start()

    def by_core(self, core):
        return self.u.at[pl.ds(core * 8, 8)]

    def quarter(self, half, at):
        return self.s1.at[pl.ds(4 * half + 2 * at, 2)]

    def eighth(self, half, at):
        return (self.sa, self.sb)[half].at[pl.ds(at, 1)]

    def result(self, half):
        return self.p.at[pl.ds(half, 1)]

    def first(self):
        self.got(0, self.rc)
        self.add(self.s1, self.by_core(self.core), self.rc)
        self.hop(1).start()
        self.hop(2).start()

    def second(self):
        self.got(1, self.ra)
        self.add(self.sa, self.quarter(0, self.x), self.ra)
        self.hop(3).start()
        self.got(2, self.rb)
        self.add(self.sb, self.quarter(1, self.y), self.rb)
        self.hop(4).start()

    def third(self):
        self.got(3, self.ta)
        self.add(self.result(0), self.eighth(0, self.y), self.ta)
        self.got(4, self.tb)
        self.add(self.result(1), self.eighth(1, self.x), self.tb)

    def reduced(self):
        for at in range(5):
            self.hop(at).wait_send()

    def kept(self, half):
        return pltpu.make_async_copy(self.p.at[pl.ds(half, 1)], self.o.at[self.mine(half)], self.loc.at[half])

    def spread1(self):
        self.hop(5).start()
        self.hop(6).start()
        self.kept(0).start()
        self.kept(1).start()

    def spread2(self):
        x, y, core = self.x, self.y, self.core
        self.kept(0).wait()
        self.got(5, self.o.at[pl.ds(core * 8 + 2 * x + 1 - y, 1)])
        self.hop(7).start()
        self.kept(1).wait()
        self.got(6, self.o.at[pl.ds(core * 8 + 4 + 2 * y + 1 - x, 1)])
        self.hop(8).start()

    def spread3(self):
        x, y, core = self.x, self.y, self.core
        self.got(7, self.o.at[pl.ds(core * 8 + 2 - 2 * x, 2)])
        self.got(8, self.o.at[pl.ds(core * 8 + 6 - 2 * y, 2)])
        self.hop(9).start()

    def everywhere(self):
        self.got(9, self.o.at[pl.ds(8 - self.core * 8, 8)])
        for at in range(5, 10):
            self.hop(at).wait_send()


class StripSum(PlaneSum):
    @staticmethod
    def reduce_scratch(shape, dtype):
        lead, rows, cols = shape
        rest = lead - 2
        shapes = [(lead, rows)] * 2
        shapes += [(count, rows // 2) for count in (2, rest, 2, rest)] + [(count, rows // 4) for count in (2, rest)]
        return [pltpu.VMEM(item + (cols // 2,), dtype) for item in shapes] + [DMA((5,)), DMA((5,))]

    def lead(self, half):
        whole = (self.u if self.u is not None else self.o).shape[0]
        return pl.ds(0, 2) if half == 0 else pl.ds(2, whole - 2)

    def strip(self, core):
        size = (self.u if self.u is not None else self.o).shape[2] // 2
        return pl.ds(pl.multiple_of(core * size, 128), size)

    def rows(self, at, parts):
        size = (self.u if self.u is not None else self.o).shape[1] // parts
        return pl.ds(pl.multiple_of(at * size, 16), size)

    def by_core(self, core):
        return self.u.at[:, :, self.strip(core)]

    def quarter(self, half, at):
        return self.s1.at[self.lead(half), self.rows(at, 2)]

    def eighth(self, half, at):
        return (self.sa, self.sb)[half].at[:, self.rows(at, 4)]

    def result(self, half):
        return self.p.at[half, pl.ds(0, 2 if half == 0 else self.u.shape[0] - 2)]

    def hop(self, at):
        if at < 5:
            return super().hop(at)
        o, x, y = self.o, self.x, self.y
        mine = lambda half: o.at[
            self.lead(half), self.rows(2 * x + y if half == 0 else 2 * y + x, 4), self.strip(self.core)
        ]
        pair = lambda half: o.at[self.lead(half), self.rows(x if half == 0 else y, 2), self.strip(self.core)]
        both = o.at[:, :, self.strip(self.core)]
        return [
            lambda: self.copy(5, self.result(0), mine(0), self.y_peer),
            lambda: self.copy(6, self.result(1), mine(1), self.x_peer),
            lambda: self.copy(7, pair(0), pair(0), self.x_peer),
            lambda: self.copy(8, pair(1), pair(1), self.y_peer),
            lambda: self.copy(9, both, both, self.chip_peer),
        ][at - 5]()

    def kept(self, half):
        x, y = self.x, self.y
        mine = self.o.at[
            self.lead(half), self.rows(2 * x + y if half == 0 else 2 * y + x, 4), self.strip(self.core)
        ]
        return pltpu.make_async_copy(self.result(half), mine, self.loc.at[half])

    def spread2(self):
        x, y, mine = self.x, self.y, self.strip(self.core)
        self.kept(0).wait()
        self.got(5, self.o.at[self.lead(0), self.rows(2 * x + 1 - y, 4), mine])
        self.hop(7).start()
        self.kept(1).wait()
        self.got(6, self.o.at[self.lead(1), self.rows(2 * y + 1 - x, 4), mine])
        self.hop(8).start()

    def spread3(self):
        mine = self.strip(self.core)
        self.got(7, self.o.at[self.lead(0), self.rows(1 - self.x, 2), mine])
        self.got(8, self.o.at[self.lead(1), self.rows(1 - self.y, 2), mine])
        self.hop(9).start()

    def everywhere(self):
        self.got(9, self.o.at[:, :, self.strip(1 - self.core)])
        for at in range(5, 10):
            self.hop(at).wait_send()


def unit_pieces(unit):
    return jax.ShapeDtypeStruct((2,) + unit.shape[1:], unit.dtype)


def line_greet(bar, me, n):
    @pl.when(me > 0)
    def _():
        pl.semaphore_signal(bar, inc=1, device_id={"tensor": me - 1}, device_id_type=MESH)

    @pl.when(me < n - 1)
    def _():
        pl.semaphore_signal(bar, inc=1, device_id={"tensor": me + 1}, device_id_type=MESH)

    return jnp.where(me > 0, 1, 0) + jnp.where(me < n - 1, 1, 0)


class LineScatter:
    def __init__(self, n, x, o, buf, tmp, send, recv):
        self.n, self.x, self.o, self.buf, self.tmp, self.send, self.recv = n, x, o, buf, tmp, send, recv
        self.me = lax.axis_index("tensor")

    @staticmethod
    def scratch(n, own, cols, dtype):
        return [
            pltpu.VMEM((2, n - 1, own, cols), dtype),
            pltpu.VMEM((2, n - 1, own, cols), dtype),
            DMA((2, n - 1)),
            DMA((2, n - 1)),
        ]

    def term(self, d, k):
        return self.n - 1 - k if d == 0 else k

    def sends(self, d, k):
        return self.me < self.n - 1 - k if d == 0 else self.me > k

    def behind(self, d):
        return self.me > 0 if d == 0 else self.me < self.n - 1

    def copy(self, d, k, first):
        return pltpu.make_async_remote_copy(
            src_ref=self.x.at[self.term(d, k)] if first else self.tmp.at[d, k],
            dst_ref=self.buf.at[d, k],
            send_sem=self.send.at[d, k],
            recv_sem=self.recv.at[d, k],
            device_id={"tensor": jnp.clip(self.me + 1 if d == 0 else self.me - 1, 0, self.n - 1)},
            device_id_type=MESH,
        )

    def landed(self, d, k):
        return pltpu.make_async_copy(self.buf.at[d, k], self.buf.at[d, k], self.recv.at[d, k])

    def begin(self, ks):
        for d in range(2):

            @pl.when(jnp.logical_not(self.behind(d)))
            def _():
                for k in ks:
                    self.copy(d, k, True).start()

    def step(self, k, which=None):
        for d in range(2):
            now = self.behind(d) & self.sends(d, k)

            @pl.when(now if which is None else now & which(d))
            def _():
                self.landed(d, k).wait()
                at = self.term(d, k)
                both = self.buf[d, k].astype(jnp.float32) + self.x[at].astype(jnp.float32)
                self.tmp[d, k] = both.astype(self.tmp.dtype)
                self.copy(d, k, False).start()

    def end(self):
        self.o[...] = self.x[self.me].astype(jnp.float32)
        for d in range(2):
            for k in range(self.n - 1):

                @pl.when(self.behind(d) & (self.me == self.term(d, k)))
                def _():
                    self.landed(d, k).wait()
                    self.o[...] += self.buf[d, k].astype(jnp.float32)

        for d in range(2):
            for k in range(self.n - 1):

                @pl.when(self.sends(d, k))
                def _():
                    self.copy(d, k, False).wait_send()


GELU_SCALE = 0.7978845608028654
GELU_CUBE = 0.044715


def feed_kernel(n, nc, heads, chunks, piece_ref, *rest):
    (token_hbm, out_ref, abias_hbm, gain_hbm, shift_hbm, up_hbm, down_hbm, bias_hbm, near_ref, cot_ref), rest = rest[:10], rest[10:]
    outs, heads_ref, rest = rest[:7], rest[7], rest[8:]
    kept_refs, rest = rest[:7], rest[7:]
    feed_ref, p1_ref, p2_ref, middle_ref, gm_ref, vec_ref, p3_ref = kept_refs
    (token_ref, abias_ref, gain_ref, shift_ref, bias_ref, osem), rest = rest[:6], rest[6:]
    leave = copies(tuple(zip(kept_refs, outs)), osem)
    (o_ref, sum_ref, att_ref, gpiece, u3, bsend, brecv, bloc), rest = rest[:8], rest[8:]
    (x_ref, up_ref, down_ref, grad_ref, wsem, asend, arecv, aloc, csend, crecv, cloc), rest = rest[:11], rest[11:]
    (held, act, gp, part, acc, buf, tmp, u1, u2), rest = rest[:9], rest[9:]
    (gsend, grecv, loc, ssend, srecv), rest = rest[:5], rest[5:]
    plane = [PlaneSum(u1, p1_ref, None, rest[:10]), PlaneSum(u2, p2_ref, None, rest[10:20])]
    out_sum = StripSum(u3, p3_ref, None, rest[20:30])
    me = lax.axis_index("tensor")
    rows, width = token_ref.shape
    wide = up_ref.shape[1]
    few = rows // chunks
    f32, low = jnp.float32, jnp.bfloat16
    ctx, dp = lax.axis_index("context"), lax.axis_index("dp")
    place, total = ctx * n + me, nc * n
    my_head = me * heads + jnp.minimum(ctx, heads - 1)
    bar = pltpu.get_barrier_semaphore()
    for shift in range(1, total):
        other = lax.rem(place + shift, total)
        pl.semaphore_signal(bar, inc=1, device_id=spread(other, AXES, (nc, n)), device_id_type=MESH)
    pl.semaphore_signal(bar, inc=1, device_id={"dp": 1 - dp}, device_id_type=MESH)
    weights_in = copies(
        (
            (token_hbm, token_ref),
            (abias_hbm, abias_ref),
            (gain_hbm, gain_ref),
            (shift_hbm, shift_ref),
            (bias_hbm, bias_ref),
            (up_hbm, up_ref),
            (down_hbm, down_ref),
        ),
        wsem,
    )
    for item in weights_in:
        item.start()

    def grad_rows(block):
        return grad_ref.at[pl.ds(pl.multiple_of(block * rows, rows), rows)]

    def grad_on(d, s):
        block = jnp.clip(me - s if d == 0 else me + s, 0, n - 1)
        return pltpu.make_async_remote_copy(
            src_ref=near_ref.at[block] if s == 1 else grad_rows(block),
            dst_ref=grad_rows(block),
            send_sem=csend.at[d, s],
            recv_sem=crecv.at[d, s],
            device_id={"tensor": jnp.clip(me + 1 if d == 0 else me - 1, 0, n - 1)},
            device_id_type=MESH,
        )

    def grad_sends(d, s):
        return (me - s >= 0) & (me < n - 1) if d == 0 else (me + s < n) & (me > 0)

    def grad_near(d):
        block = jnp.clip(me - 1 if d == 0 else me + 1, 0, n - 1)
        return pltpu.make_async_copy(near_ref.at[block], grad_rows(block), cloc.at[d])

    def grad_own():
        return pltpu.make_async_copy(cot_ref, grad_rows(me), cloc.at[2])

    def beside(d):
        return me > 0 if d == 0 else me < n - 1

    grad_own().start()
    for d in range(2):

        @pl.when(beside(d))
        def _():
            grad_near(d).start()

    pl.semaphore_wait(bar, total)
    for d in range(2):

        @pl.when(grad_sends(d, 1))
        def _():
            grad_on(d, 1).start()

    def to_place(shift):
        other = lax.rem(place + shift, total)
        return pltpu.make_async_remote_copy(
            src_ref=piece_ref.at[other],
            dst_ref=att_ref.at[my_head],
            send_sem=asend.at[shift],
            recv_sem=arecv.at[shift],
            device_id=spread(other, AXES, (nc, n)),
            device_id_type=MESH,
        )

    @pl.when(ctx < heads)
    def _():
        for shift in range(1, total):
            to_place(shift).start()
        stay = pltpu.make_async_copy(piece_ref.at[place], att_ref.at[my_head], aloc)
        stay.start()
        stay.wait()

    for shift in range(1, total):
        source = lax.rem(place + total - shift, total)
        at_ctx, at_ten = lax.div(source, n), lax.rem(source, n)

        @pl.when(at_ctx < heads)
        def _():
            landed = att_ref.at[at_ten * heads + jnp.minimum(at_ctx, heads - 1)]
            pltpu.make_async_copy(landed, landed, arecv.at[shift]).wait()

    for item in weights_in[:4]:
        item.wait()
    attended = att_ref[...].reshape(width, rows)
    middle = token_ref[...].astype(f32) + dot(attended, out_ref[...], ((0,), (0,))) + row(abias_ref)
    middle_ref[...] = middle
    leave[3].start()
    x_ref[...] = (norm_parts(middle)[0] * row(gain_ref) + row(shift_ref)).astype(low)

    @pl.when(ctx < heads)
    def _():
        for shift in range(1, total):
            to_place(shift).wait_send()

    def rows_of(block):
        return pl.ds(pl.multiple_of(block * rows, rows), rows)

    def neighbour(d):
        return {"tensor": jnp.clip(jnp.where(d == 0, me + 1, me - 1), 0, n - 1)}

    def onward(d):
        return jnp.where(d == 0, me, n - 1 - me) < n - 1

    def hand_on(d, s, block, first):
        return pltpu.make_async_remote_copy(
            src_ref=x_ref if first else held.at[rows_of(block)],
            dst_ref=held.at[rows_of(block)],
            send_sem=gsend.at[d, s],
            recv_sem=grecv.at[d, s],
            device_id=neighbour(d),
            device_id_type=MESH,
        )

    def chunk(block, c):
        return pl.ds(pl.multiple_of(block * rows + c * few, few), few)

    def back(d, block, c, first):
        at = chunk(block, c)
        return pltpu.make_async_remote_copy(
            src_ref=part.at[at] if first else tmp.at[at],
            dst_ref=buf.at[d, at],
            send_sem=ssend.at[block, c],
            recv_sem=srecv.at[d, block, c],
            device_id=neighbour(d),
            device_id_type=MESH,
        )

    for d in range(2):

        @pl.when(onward(d))
        def _():
            hand_on(d, 0, me, True).start()

    own = pltpu.make_async_copy(x_ref, held.at[rows_of(me)], loc)
    own.start()
    sum_ref[...] = jnp.zeros_like(sum_ref)
    own.wait()
    for item in weights_in[4:]:
        item.wait()
    grad_own().wait()
    for d in range(2):

        @pl.when(beside(d))
        def _():
            grad_near(d).wait()

    for s in range(1, n - 1):
        for d in range(2):
            block = me - 1 - s if d == 0 else me + 1 + s

            @pl.when((block >= 0) & (block < n))
            def _():
                landed = grad_rows(jnp.clip(block, 0, n - 1))
                pltpu.make_async_copy(landed, landed, crecv.at[d, s]).wait()

            if s + 1 < n - 1:

                @pl.when(grad_sends(d, s + 1))
                def _():
                    grad_on(d, s + 1).start()

        if s == n - 3:
            break
    columns = 256

    def work(block):
        here = rows_of(block)
        acc[...] = jnp.zeros_like(acc)

        @pl.loop(0, wide // columns)
        def _(j):
            at = pl.ds(pl.multiple_of(j * columns, columns), columns)
            pre = dot(held[here, :], up_ref[:, at], ((1,), (0,))) + bias_ref[at].reshape(1, -1)
            square = pre * pre
            tanh = jnp.tanh(GELU_SCALE * pre * (1.0 + GELU_CUBE * square))
            act[here, at] = (0.5 * pre * (1.0 + tanh)).astype(low)
            slope = 0.5 * (1.0 + tanh) + 0.5 * pre * (1.0 - tanh * tanh) * (
                GELU_SCALE * (1.0 + 3.0 * GELU_CUBE * square)
            )
            grad = (dot(grad_ref[here, :], down_ref[at, :], ((1,), (1,))) * slope).astype(low)
            gp[here, at] = grad
            acc[...] += dot(grad, up_ref[:, at], ((1,), (1,)))

        part[here, :] = acc[...].astype(low)
        sum_ref[...] += jnp.sum(gp[here, :].astype(f32), axis=0, keepdims=True)

    near = jnp.minimum(me, n - 1 - me)
    toward = jnp.where(2 * me < n - 1, -1, 1)

    @pl.loop(0, n)
    def _(slot):
        paired = slot <= 2 * near
        distance = jnp.where(paired, lax.div(slot + 1, 2), slot - near)
        side = jnp.where(paired & (lax.rem(slot, 2) == 1), toward, -toward)
        block = me + side * distance
        d = jnp.where(block < me, 0, 1)
        s = jnp.maximum(distance - 1, 0)

        @pl.when(slot > 0)
        def _():
            landed = held.at[rows_of(block)]
            pltpu.make_async_copy(landed, landed, grecv.at[d, s]).wait()

            @pl.when(onward(d))
            def _():
                hand_on(d, jnp.minimum(s + 1, n - 2), block, False).start()

        @pl.when(distance == n - 1)
        def _():
            landed = grad_rows(block)
            pltpu.make_async_copy(landed, landed, crecv.at[d, n - 2]).wait()

        work(block)

        @pl.when((slot > 0) & ((me == 0) | (me == n - 1)))
        def _():
            for c in range(chunks):
                back(1 - d, block, c, True).start()

    def weights(left, right, unit):
        half = wide // 2

        @pl.loop(0, 2)
        def _(j):
            at = pl.ds(pl.multiple_of(j * half, 128), half)
            total = dot(left[:, at], right[...], ((0,), (0,)))
            unit[pl.ds(8 * j, 8)] = total.astype(low).reshape((8,) + unit.shape[1:])

    weights(act, grad_ref, u1)
    plane[0].begin()
    weights(held, gp, u2)
    plane[1].begin()

    def relay(way, block):
        d = jnp.where(way > 0, 0, 1)

        @pl.when((me > 0) & (me < n - 1) & (block >= 0) & (block < n))
        def _():
            for c in range(chunks):
                at = chunk(block, c)
                landed = buf.at[d, at]
                pltpu.make_async_copy(landed, landed, srecv.at[d, block, c]).wait()
                tmp[at, :] = (buf[d, at, :].astype(f32) + part[at, :].astype(f32)).astype(low)
                back(d, block, c, False).start()

    plane[0].first()
    for j in range(1, n):
        relay(-toward, me - toward * j)
        if j == 1:
            plane[1].first()

    @pl.loop(0, n)
    def _(block):
        here = rows_of(block)
        feed_ref[here, :] = dot(act[here, :], down_ref[...], ((1,), (0,))).astype(low)

    leave[0].start()

    plane[0].second()
    plane[1].second()
    for j in range(1, n):
        relay(toward, me + toward * j)
    for item in plane:
        item.third()
    for c in range(chunks):
        at = chunk(me, c)
        mine = pl.ds(c * few, few)
        o_ref[mine, :] = part[at, :].astype(f32)
        for d in range(2):

            @pl.when(me > 0 if d == 0 else me < n - 1)
            def _():
                landed = buf.at[d, at]
                pltpu.make_async_copy(landed, landed, srecv.at[d, me, c]).wait()
                o_ref[mine, :] += buf[d, at, :].astype(f32)

    grad = o_ref[...]
    normed, scale = norm_parts(middle_ref[...])
    above = grad_ref[rows_of(me), :].astype(f32)
    grad_middle = above + norm_backward(grad, normed, scale, row(gain_ref))
    gm_ref[...] = grad_middle
    for at in (1, 2, 4):
        leave[at].start()
    gm_low = grad_middle.astype(low)
    back_out = dot(out_ref[...], gm_low, ((1,), (1,))).astype(low)
    gpiece[...] = back_out.reshape(gpiece.shape)
    vec_ref[...] = jnp.zeros_like(vec_ref)
    vec_ref[2:3, :] = jnp.sum(gm_low.astype(f32), axis=0, keepdims=True)

    def to_head(shift):
        other = lax.rem(place + shift, total)
        at_ctx, at_ten = lax.div(other, n), lax.rem(other, n)
        return at_ctx < heads, pltpu.make_async_remote_copy(
            src_ref=gpiece.at[at_ten * heads + jnp.minimum(at_ctx, heads - 1)],
            dst_ref=heads_ref.at[place],
            send_sem=bsend.at[shift],
            recv_sem=brecv.at[shift],
            device_id={"context": at_ctx, "tensor": at_ten},
            device_id_type=MESH,
        )

    for shift in range(1, total):
        goes, item = to_head(shift)

        @pl.when(goes)
        def _():
            item.start()

    stay = pltpu.make_async_copy(gpiece.at[my_head], heads_ref.at[place], bloc)
    stay.start()
    u3[...] = dot(att_ref[...].reshape(width, rows), gm_low, ((1,), (0,))).astype(low).reshape(u3.shape)
    out_sum.begin()
    vec_ref[3:4, :] = jnp.sum(grad * normed, axis=0, keepdims=True)
    vec_ref[4:5, :] = jnp.sum(grad, axis=0, keepdims=True)
    vec_ref[5:6, :] = jnp.sum(above, axis=0, keepdims=True)
    vec_ref[6:7, :] = sum_ref[...]
    out_sum.first()
    out_sum.second()
    out_sum.third()
    leave[5].start()
    leave[6].start()
    stay.wait()

    @pl.when(ctx < heads)
    def _():
        for shift in range(1, total):
            source = lax.rem(place + total - shift, total)
            landed = heads_ref.at[source]
            pltpu.make_async_copy(landed, landed, brecv.at[shift]).wait()

    for shift in range(1, total):
        goes, item = to_head(shift)

        @pl.when(goes)
        def _():
            item.wait_send()

    out_sum.reduced()
    for item in leave:
        item.wait()
    for d in range(2):
        for s in range(n - 1):
            block = me - s if d == 0 else me + s

            @pl.when(onward(d) & (block >= 0) & (block < n))
            def _():
                hand_on(d, s, me, True).wait_send()

    for block in range(n):

        @pl.when(me != block)
        def _():
            for c in range(chunks):
                back(jnp.where(me < block, 0, 1), block, c, True).wait_send()

    for d in range(2):
        for s in range(1, n - 1):

            @pl.when(grad_sends(d, s))
            def _():
                grad_on(d, s).wait_send()

    for item in plane:
        item.reduced()


def feed_part(pieces, tokens, out_weight, vectors, up, down, bias, near, cotangent, n, nc, heads, collective_id):
    rows, width = tokens.shape
    wide = up.shape[1]
    chunks = 2
    total = n * rows
    low, f32 = jnp.bfloat16, jnp.float32
    unit = (16, wide // 16, width)
    piece = jax.ShapeDtypeStruct((2,) + unit[1:], low)
    return pl.pallas_call(
        functools.partial(feed_kernel, n, nc, heads, chunks),
        out_shape=(
            jax.ShapeDtypeStruct((total, width), low),
            piece,
            piece,
            jax.ShapeDtypeStruct((rows, width), f32),
            jax.ShapeDtypeStruct((rows, width), f32),
            jax.ShapeDtypeStruct((8, width), f32),
            jax.ShapeDtypeStruct((2, 2, rows // 4, width // 2), low),
            jax.ShapeDtypeStruct(pieces.shape, low),
        ),
        in_specs=[VM, HB, VM, HB, HB, HB, HB, HB, HB, VM, HB],
        out_specs=(HB,) * 7 + (VM,),
        scratch_shapes=[
            pltpu.VMEM((total, width), low),
            pltpu.VMEM(piece.shape, low),
            pltpu.VMEM(piece.shape, low),
            pltpu.VMEM((rows, width), f32),
            pltpu.VMEM((rows, width), f32),
            pltpu.VMEM((8, width), f32),
            pltpu.VMEM((2, 2, rows // 4, width // 2), low),
            pltpu.VMEM(tokens.shape, tokens.dtype),
            pltpu.VMEM((width,), f32),
            pltpu.VMEM((width,), f32),
            pltpu.VMEM((width,), f32),
            pltpu.VMEM((wide,), f32),
            DMA((7,)),
            pltpu.VMEM((rows, width), f32),
            pltpu.VMEM((1, wide), f32),
            pltpu.VMEM((n * heads,) + pieces.shape[1:], low),
            pltpu.VMEM((n * heads,) + pieces.shape[1:], low),
            pltpu.VMEM((n, width // n, width), low),
            DMA((nc * n,)),
            DMA((nc * n,)),
            DMA,
            pltpu.VMEM((rows, width), low),
            pltpu.VMEM(up.shape, low),
            pltpu.VMEM(down.shape, low),
            pltpu.VMEM((total, width), low),
            DMA((7,)),
            DMA((nc * n,)),
            DMA((nc * n,)),
            DMA,
            DMA((2, n - 1)),
            DMA((2, n - 1)),
            DMA((3,)),
            pltpu.VMEM((total, width), low),
            pltpu.VMEM((total, wide), low),
            pltpu.VMEM((total, wide), low),
            pltpu.VMEM((total, width), low),
            pltpu.VMEM((rows, width), f32),
            pltpu.VMEM((2, total, width), low),
            pltpu.VMEM((total, width), low),
            pltpu.VMEM(unit, low),
            pltpu.VMEM(unit, low),
            DMA((2, n - 1)),
            DMA((2, n - 1)),
            DMA,
            DMA((n, chunks)),
            DMA((2, n, chunks)),
        ]
        + PlaneSum.reduce_scratch(unit, low) * 2
        + StripSum.reduce_scratch((n, width // n, width), low),
        compiler_params=remote_params(collective_id, 40),
    )(pieces, tokens, out_weight, *vectors, up, down, bias, near, cotangent)


def last_kernel(n, nc, heads, shared, count, x_ref, w_hbm, h_hbm, a_hbm, feed_hbm, mid_hbm, bias_hbm, *rest):
    ps, rest = rest[:count], rest[count:]
    (token_hbm, gain_hbm, middle_hbm, vec_hbm), rest = rest[:4], rest[4:]
    (out_ref, g_ref, v_ref, po_ref, ao_ref), rest = rest[:5], rest[5:]
    outs, rest = rest[:count], rest[count:]
    (rows_ref, w_ref, h_ref, token_ref, middle_ref, part, sum_ref, u_ref, piece), rest = rest[:9], rest[9:]
    (hsend, hrecv, hloc, win), rest = rest[:4], rest[4:]
    (feed_ref, fsum_ref, mid_ref, bias_ref, gain_ref, vec_ref), rest = rest[:6], rest[6:]
    feed_line = LineScatter(n, feed_ref, fsum_ref, *rest[:4])
    rest = rest[4:]
    chunks = 2
    own = token_ref.shape[0]
    few = own // chunks
    lines = [
        LineScatter(n, part.at[:, pl.ds(c * few, few)], sum_ref.at[pl.ds(c * few, few)], *rest[4 * c : 4 * c + 4])
        for c in range(chunks)
    ]
    rest = rest[4 * chunks :]
    project = StripSum(u_ref, piece, po_ref, rest[:10], rest[10:13])
    rest = rest[13:]
    feeds = [PlaneSum(None, ps[i], outs[i], None, rest[3 * i : 3 * i + 3]) for i in range(count)]
    rest = rest[3 * count :]
    (land, zsend, zrecv, zloc, a_ref), rest = rest[:5], rest[5:]
    (asend, arecv, aloc, now), rest = rest[:4], rest[4:]
    sizes = (n, 2 * nc)
    bufs, sems = rest[:2], rest[2:]
    f32, low = jnp.float32, jnp.bfloat16

    ten, ctx, x = (lax.axis_index(name) for name in ("tensor", "context", "dp"))
    place = ctx * 2 + x
    bar = pltpu.get_barrier_semaphore()
    for shift in range(1, n):
        pl.semaphore_signal(bar, inc=1, device_id={"tensor": lax.rem(ten + shift, n)}, device_id_type=MESH)
    for shift in range(1, 8):
        other = lax.rem(place + shift, 8)
        pl.semaphore_signal(
            bar, inc=1, device_id={"context": lax.div(other, 2), "dp": lax.rem(other, 2)}, device_id_type=MESH
        )
    copies_in = copies(
        (
            (feed_hbm, feed_ref),
            (token_hbm, token_ref),
            (w_hbm, w_ref),
            (h_hbm, h_ref),
            (middle_hbm, middle_ref),
            (mid_hbm, mid_ref),
            (bias_hbm, bias_ref),
            (gain_hbm, gain_ref),
            (vec_hbm, vec_ref),
        ),
        win,
    )
    for item in copies_in:
        item.start()
    pl.semaphore_wait(bar, n + 6)

    half = 2 * own
    far = 1 - lax.div(ten, 2)
    pairs = (far, 1 - far)

    def columns(pair):
        return pl.ds(pl.multiple_of(pair * half, 128), half)

    def ship(index, shift):
        other = lax.rem(ctx + shift, nc)
        return pltpu.make_async_remote_copy(
            src_ref=x_ref.at[other, :, :, columns(pairs[index])],
            dst_ref=rows_ref.at[:, jnp.minimum(ctx, heads - 1), :, columns(pairs[index])],
            send_sem=hsend.at[index, shift],
            recv_sem=hrecv.at[index, shift],
            device_id={"context": other},
            device_id_type=MESH,
        )

    @pl.when(ctx < heads)
    def _():
        for index in range(2):
            for shift in range(1, nc):
                ship(index, shift).start()
        stay = pltpu.make_async_copy(x_ref.at[ctx], rows_ref.at[:, ctx], hloc)
        stay.start()
        stay.wait()

    def across(shift):
        other = lax.rem(ten + shift, n)
        return pltpu.make_async_remote_copy(
            src_ref=a_hbm.at[lax.div(other, 2), lax.rem(other, 2)],
            dst_ref=land.at[ten],
            send_sem=zsend.at[shift],
            recv_sem=zrecv.at[shift],
            device_id={"tensor": other},
            device_id_type=MESH,
        )

    copies_in[0].wait()
    feed_line.begin((0, 1))
    for shift in range(1, n):
        across(shift).start()
    mine = pltpu.make_async_copy(a_hbm.at[lax.div(ten, 2), lax.rem(ten, 2)], land.at[ten], zloc)
    mine.start()
    for item in feeds:
        item.spread1()

    def there(at):
        ctx_, x_ = lax.div(at, 2), lax.rem(at, 2)
        y_ = lax.div(ctx_, 2)
        row_ = jnp.where(ten < n // 2, 2 * x_ + y_, 2 * y_ + x_)
        rows = pl.ds(pl.multiple_of(row_ * a_ref.shape[0], 16), a_ref.shape[0])
        cols = pl.ds(pl.multiple_of(lax.rem(ctx_, 2) * a_ref.shape[1], 128), a_ref.shape[1])
        return ao_ref.at[rows, cols]

    def push(shift):
        other = lax.rem(place + shift, 8)
        return pltpu.make_async_remote_copy(
            src_ref=a_ref,
            dst_ref=there(place),
            send_sem=asend.at[shift],
            recv_sem=arecv.at[shift],
            device_id={"context": lax.div(other, 2), "dp": lax.rem(other, 2)},
            device_id_type=MESH,
        )

    copies_in[1].wait()
    normed, scale = norm_parts(token_ref[...].astype(f32))
    mine.wait()
    for shift in range(1, n):
        source = lax.rem(ten + n - shift, n)
        pltpu.make_async_copy(land.at[source], land.at[source], zrecv.at[shift]).wait()
    value = land[0].astype(f32)
    for at in range(1, n):
        value = value + land[at].astype(f32)
    a_ref[...] = value.astype(low)
    for item in copies_in[2:]:
        item.wait()
    now[0] = vec_ref[...]
    for shift in range(1, 8):
        push(shift).start()
    kept = pltpu.make_async_copy(a_ref, there(place), aloc)
    kept.start()

    def partials(index):
        at = columns(pairs[index])
        for shift in range(1, nc):
            source = lax.rem(ctx + nc - shift, nc)

            @pl.when(source < heads)
            def _():
                ref = rows_ref.at[:, jnp.minimum(source, heads - 1), :, at]
                pltpu.make_async_copy(ref, ref, hrecv.at[index, shift]).wait()

        total = 0.0
        for kind in range(3):
            grads = rows_ref[kind, :, :, at].reshape(heads * HEAD_DIM, half)
            total = total + dot(grads, w_ref[kind], ((0,), (0,)))
        part[pl.ds(2 * pairs[index], 2)] = total.astype(low).reshape(2, own, total.shape[1])

    first = lambda d: (ten < n // 2) if d == 0 else (ten >= n // 2)
    second = lambda d: (ten >= n // 2) if d == 0 else (ten < n // 2)
    feed_line.step(0, first)
    partials(0)
    for line in lines:
        line.begin((0, 1))
    partials(1)
    for line in lines:
        line.begin((2,))
    feed_line.begin((2,))
    for item in feeds:
        item.spread2()
    for line in lines:
        line.step(0, first)
    feed_line.step(1, first)
    feed_line.step(0, second)
    for kind in range(3):
        grads = rows_ref[kind].reshape(heads * HEAD_DIM, n * own)
        u_ref[kind] = dot(grads, h_ref[...], ((1,), (0,))).astype(low)
    project.begin()
    for line in lines:
        line.step(1, first)
    ends = jnp.concatenate(
        [rows_ref[kind].reshape(heads * HEAD_DIM, n * own) for kind in (0, 2)], axis=0
    )
    bias = dot(jnp.ones((8, n * own), low), ends, ((1,), (1,)))
    now[0, 7:8, 0 : bias.shape[1]] = bias[0:1]
    project.first()
    for item in feeds:
        item.spread3()
    project.second()
    for k in range(n - 1):
        for line in lines:
            line.step(k, second)
    feed_line.step(1, second)
    project.third()
    project.spread1()
    for line in lines:
        line.end()
    grad = sum_ref[...]
    now[0, 0:1] = jnp.sum(grad * normed, axis=0, keepdims=True)
    now[0, 1:2] = jnp.sum(grad, axis=0, keepdims=True)
    alone = now[0]

    def where(stage):
        return ten if stage == 0 else place

    def stage_copy(stage, shift):
        other = lax.rem(where(stage) + shift, sizes[stage])
        peer = {"tensor": other} if stage == 0 else {"context": lax.div(other, 2), "dp": lax.rem(other, 2)}
        return pltpu.make_async_remote_copy(
            src_ref=now.at[stage],
            dst_ref=bufs[stage].at[where(stage)],
            send_sem=sems[2 * stage].at[shift],
            recv_sem=sems[2 * stage + 1].at[shift],
            device_id=peer,
            device_id_type=MESH,
        )

    def stage_start(stage):
        for shift in range(1, sizes[stage]):
            stage_copy(stage, shift).start()
        bufs[stage][where(stage)] = now[stage]

    def stage_end(stage):
        buf, size = bufs[stage], sizes[stage]
        for shift in range(1, size):
            source = lax.rem(where(stage) + size - shift, size)
            pltpu.make_async_copy(buf.at[source], buf.at[source], sems[2 * stage + 1].at[shift]).wait()
        total = buf[0]
        for at in range(1, size):
            total = total + buf[at]
        if stage == 0:
            line_ = lax.broadcasted_iota(jnp.int32, total.shape, 0)
            now[1] = jnp.where(line_ < shared, total, alone)
        else:
            v_ref[...] = total

    stage_start(0)
    back = norm_backward(grad, normed, scale, row(gain_ref))
    g_ref[...] = (middle_ref[...] + back).astype(g_ref.dtype)
    project.spread2()
    stage_end(0)
    stage_start(1)
    project.spread3()
    feed_line.end()
    out_ref[...] = (mid_ref[...] + fsum_ref[...] + row(bias_ref)).astype(low)
    kept.wait()
    for shift in range(1, 8):
        source = there(lax.rem(place + 8 - shift, 8))
        pltpu.make_async_copy(source, source, arecv.at[shift]).wait()
    for item in feeds:
        item.everywhere()
    stage_end(1)
    project.everywhere()
    project.reduced()

    @pl.when(ctx < heads)
    def _():
        for index in range(2):
            for shift in range(1, nc):
                ship(index, shift).wait_send()

    for shift in range(1, n):
        across(shift).wait_send()
    for shift in range(1, 8):
        push(shift).wait_send()
    for stage in range(2):
        for shift in range(1, sizes[stage]):
            stage_copy(stage, shift).wait_send()


def last_part(x, weight, hidden, attend_pieces, feed, middle, bias, pieces, tokens, gain, grad_middle, vectors, shared, n, heads, collective_id):
    nc = x.shape[0]
    own, cols = tokens.shape
    count = len(pieces)
    f32, low = jnp.float32, jnp.bfloat16
    whole = lambda item: jax.ShapeDtypeStruct((16,) + item.shape[1:], item.dtype)
    wide, deep = attend_pieces.shape[2:]
    unit = (3, heads * HEAD_DIM, cols)
    result = pl.pallas_call(
        functools.partial(last_kernel, n, nc, heads, shared, count),
        out_shape=(
            jax.ShapeDtypeStruct((own, cols), low),
            jax.ShapeDtypeStruct((own, cols), low),
            jax.ShapeDtypeStruct(vectors.shape, f32),
            jax.ShapeDtypeStruct(unit, low),
            jax.ShapeDtypeStruct((4 * wide, 2 * deep), low),
        )
        + tuple(whole(item) for item in pieces),
        in_specs=[VM] + [HB] * (10 + count),
        out_specs=(VM,) * (5 + count),
        scratch_shapes=[
            pltpu.VMEM((3, heads, HEAD_DIM, n * own), low),
            pltpu.VMEM(weight.shape, low),
            pltpu.VMEM(hidden.shape, low),
            pltpu.VMEM(tokens.shape, low),
            pltpu.VMEM((own, cols), f32),
            pltpu.VMEM((n, own, cols), low),
            pltpu.VMEM((own, cols), f32),
            pltpu.VMEM(unit, low),
            pltpu.VMEM((2, 2, unit[1] // 4, cols // 2), low),
            DMA((2, nc)),
            DMA((2, nc)),
            DMA,
            DMA((9,)),
            pltpu.VMEM((n, own, cols), low),
            pltpu.VMEM((own, cols), f32),
            pltpu.VMEM((own, cols), f32),
            pltpu.VMEM((cols,), f32),
            pltpu.VMEM((cols,), f32),
            pltpu.VMEM(vectors.shape, f32),
        ]
        + LineScatter.scratch(n, own, cols, low)
        + LineScatter.scratch(n, own // 2, cols, low) * 2
        + StripSum.reduce_scratch(unit, low)
        + PlaneSum.spread_scratch()
        + [item for _ in pieces for item in PlaneSum.spread_scratch()]
        + [pltpu.VMEM((n, wide, deep), low), DMA((n,)), DMA((n,)), DMA, pltpu.VMEM((wide, deep), low)]
        + [DMA((8,)), DMA((8,)), DMA, pltpu.VMEM((2,) + vectors.shape, f32)]
        + [pltpu.VMEM((size,) + vectors.shape, f32) for size in (n, 2 * nc)]
        + [DMA((size,)) for size in (n, 2 * nc) for _ in range(2)],
        compiler_params=remote_params(collective_id, 32),
    )(
        x, weight, hidden, attend_pieces, feed.reshape(n, own, cols), middle, bias,
        *pieces, tokens, gain, grad_middle, vectors,
    )
    return result[:5] + (result[5:],)


class LineGather:
    def __init__(self, n, x, o, send, recv):
        self.n, self.x, self.o, self.send, self.recv = n, x, o, send, recv
        self.me = lax.axis_index("tensor")

    def copy(self, d, s):
        me, n = self.me, self.n
        shard = jnp.clip(me - s if d == 0 else me + s, 0, n - 1)
        return pltpu.make_async_remote_copy(
            src_ref=self.x if s == 0 else self.o.at[shard],
            dst_ref=self.o.at[shard],
            send_sem=self.send.at[d, s],
            recv_sem=self.recv.at[d, s],
            device_id={"tensor": jnp.clip(me + 1 if d == 0 else me - 1, 0, n - 1)},
            device_id_type=MESH,
        )

    def sends(self, d, s):
        me, n = self.me, self.n
        return (me - s >= 0) & (me < n - 1) if d == 0 else (me + s < n) & (me > 0)

    def wait(self, d, s):
        me, n = self.me, self.n

        @pl.when(me - 1 - s >= 0 if d == 0 else me + 1 + s < n)
        def _():
            shard = jnp.clip(me - 1 - s if d == 0 else me + 1 + s, 0, n - 1)
            pltpu.make_async_copy(self.o.at[shard], self.o.at[shard], self.recv.at[d, s]).wait()

    def step(self, s):
        for d in range(2):
            if s > 0:
                self.wait(d, s - 1)

            @pl.when(self.sends(d, s))
            def _():
                self.copy(d, s).start()

    def last(self):
        for d in range(2):
            self.wait(d, self.n - 2)

    def finish(self, steps=None):
        for d in range(2):
            for s in range(steps or self.n - 1):

                @pl.when(self.sends(d, s))
                def _():
                    self.copy(d, s).wait_send()


def start_kernel(n, nc, heads, t_hbm, gain_hbm, shift_hbm, full_ref, w_hbm, b_hbm, c_ref, o_hbm, f_ref, q_ref, g_ref, *rest):
    (x_ref, held, proj, w_ref, o_ref, t_ref, gain_ref, shift_ref, b_ref, win), rest = rest[:10], rest[10:]
    arrive = copies(((t_hbm, t_ref), (gain_hbm, gain_ref), (shift_hbm, shift_ref), (b_hbm, b_ref)), win)
    for item in arrive:
        item.start()
    s1, r1, s2, r2, s5, r5, s3, r3, s4, r4, loc = rest
    me, ctx, x = lax.axis_index("tensor"), lax.axis_index("context"), lax.axis_index("dp")
    core, y = lax.rem(ctx, 2), lax.div(ctx, 2)
    rows, width = t_ref.shape
    half = 2 * rows
    bar = pltpu.get_barrier_semaphore()
    met = line_greet(bar, me, n)
    for shift in range(1, nc):
        pl.semaphore_signal(bar, inc=1, device_id={"context": lax.rem(ctx + shift, nc)}, device_id_type=MESH)
    pl.semaphore_signal(bar, inc=1, device_id={"dp": 1 - x}, device_id_type=MESH)
    weight_in = pltpu.make_async_copy(w_hbm, w_ref, loc.at[4])
    weight_in.start()
    for item in arrive:
        item.wait()
    normed, _ = norm_parts(t_ref[...].astype(jnp.float32))
    x_ref[...] = (normed * row(gain_ref) + row(shift_ref)).astype(x_ref.dtype)
    pl.semaphore_wait(bar, met + nc)

    tall, deep = held.shape[1:]
    strip = pl.ds(pl.multiple_of(core * deep, 128), deep)
    piece = full_ref.at[pl.ds(pl.multiple_of((2 * y + x) * tall, 16), tall), strip]
    small = LineGather(n, piece, held, s1, r1)
    large = LineGather(n, x_ref, o_ref, s2, r2)
    grads = LineGather(n, c_ref, g_ref, s5, r5)
    small.step(0)
    large.step(0)
    own = pltpu.make_async_copy(x_ref, o_ref.at[me], loc.at[0])
    own.start()
    mine = pltpu.make_async_copy(piece, held.at[me], loc.at[1])
    mine.start()
    mine.wait()
    own.wait()
    for s in range(1, n - 1):
        small.step(s)
    small.last()

    def there(y_, x_):
        return f_ref.at[:, pl.ds(pl.multiple_of((2 * y_ + x_) * tall, 16), tall), strip]

    x_peer, y_peer = {"dp": 1 - x}, {"context": lax.rem(ctx + 2, 4)}

    def hop(at):
        src, dst, peer = [
            (held, there(y, x), x_peer),
            (held, there(y, x), y_peer),
            (there(y, 1 - x), there(y, 1 - x), y_peer),
            (f_ref.at[:, :, strip], f_ref.at[:, :, strip], {"context": ctx + 1 - 2 * core}),
        ][at]
        return pltpu.make_async_remote_copy(
            src_ref=src,
            dst_ref=dst,
            send_sem=s3.at[at],
            recv_sem=r3.at[at],
            device_id=peer,
            device_id_type=MESH,
        )

    def got(at):
        other = pl.ds(pl.multiple_of((1 - core) * deep, 128), deep)
        ref = [there(y, 1 - x), there(1 - y, x), there(1 - y, 1 - x), f_ref.at[:, :, other]][at]
        pltpu.make_async_copy(ref, ref, r3.at[at]).wait()

    hop(0).start()
    kept = pltpu.make_async_copy(held, there(y, x), loc.at[2])
    kept.start()

    def columns(pair):
        return pl.ds(pl.multiple_of(pair * half, 128), half)

    def project(pair):
        token = jnp.concatenate([o_ref[2 * pair], o_ref[2 * pair + 1]], axis=0)
        for kind in range(3):
            value = dot(w_ref[kind], token, ((1,), (1,))) + b_ref[kind]
            proj[kind, :, :, columns(pair)] = value.astype(proj.dtype).reshape(heads, HEAD_DIM, half)

    def ship(index, pair, shift):
        other = lax.rem(ctx + shift, nc)
        return other, pltpu.make_async_remote_copy(
            src_ref=proj.at[:, jnp.minimum(other, heads - 1), :, columns(pair)],
            dst_ref=q_ref.at[ctx, :, :, columns(pair)],
            send_sem=s4.at[index, shift],
            recv_sem=r4.at[index, shift],
            device_id={"context": other},
            device_id_type=MESH,
        )

    def ship_all(index, pair):
        for shift in range(1, nc):
            other, item = ship(index, pair, shift)

            @pl.when(other < heads)
            def _():
                item.start()

    near = lax.div(me, 2)
    large.step(1)
    weight_in.wait()
    project(near)
    ship_all(0, near)
    hop(1).start()
    for s in range(2, n - 1):
        large.step(s)
    grads.step(0)
    got(0)
    hop(2).start()
    large.last()
    project(1 - near)
    ship_all(1, 1 - near)
    result = pltpu.make_async_copy(o_ref, o_hbm, loc.at[5])
    result.start()
    stay = pltpu.make_async_copy(proj.at[:, jnp.minimum(ctx, heads - 1)], q_ref.at[ctx], loc.at[3])
    stay.start()
    kept.wait()
    got(1)
    got(2)
    hop(3).start()
    stay.wait()

    @pl.when(ctx < heads)
    def _():
        for index in range(2):
            for shift in range(1, nc):
                source = lax.rem(ctx + nc - shift, nc)
                pair = near if index == 0 else 1 - near
                ref = q_ref.at[source, :, :, columns(pair)]
                pltpu.make_async_copy(ref, ref, r4.at[index, shift]).wait()

    got(3)
    for d in range(2):
        grads.wait(d, 0)
    result.wait()
    small.finish()
    large.finish()
    grads.finish(1)
    for at in range(4):
        hop(at).wait_send()
    for index in range(2):
        for shift in range(1, nc):
            other, item = ship(index, near if index == 0 else 1 - near, shift)

            @pl.when(other < heads)
            def _():
                item.wait_send()


def start_part(tokens, gain, shift, w, project_weight, bias, cotangent, n, nc, heads, collective_id):
    rows, cols = tokens.shape
    wide, deep = w.shape
    low = jnp.bfloat16
    full, weight, qkv, grads = pl.pallas_call(
        functools.partial(start_kernel, n, nc, heads),
        out_shape=(
            jax.ShapeDtypeStruct((n, rows, cols), low),
            jax.ShapeDtypeStruct((n, wide, deep), w.dtype),
            jax.ShapeDtypeStruct((nc, 3, HEAD_DIM, n * rows), low),
            jax.ShapeDtypeStruct((n, rows, cols), low),
        ),
        in_specs=[HB] * 7,
        out_specs=(HB, VM, VM, VM),
        scratch_shapes=[
            pltpu.VMEM((rows, cols), low),
            pltpu.VMEM((n, wide // 4, deep // 2), w.dtype),
            pltpu.VMEM((3, heads, HEAD_DIM, n * rows), low),
            pltpu.VMEM(project_weight.shape, low),
            pltpu.VMEM((n, rows, cols), low),
            pltpu.VMEM((rows, cols), tokens.dtype),
            pltpu.VMEM(gain.shape, jnp.float32),
            pltpu.VMEM(shift.shape, jnp.float32),
            pltpu.VMEM(bias.shape, jnp.float32),
            DMA((4,)),
        ]
        + [DMA((2, n - 1)) for _ in range(6)]
        + [DMA((4,)), DMA((4,)), DMA((2, nc)), DMA((2, nc)), DMA((6,))],
        compiler_params=remote_params(collective_id),
    )(tokens, gain, shift, w, project_weight, bias, cotangent)
    return full.reshape(n * rows, cols), weight.reshape(n * wide, deep), qkv, grads


def dot(left, right, dims):
    return lax.dot_general(left, right, ((dims[0], dims[1]), ((), ())), preferred_element_type=jnp.float32)


def key_positions(first, keys, queries):
    return first + lax.broadcasted_iota(jnp.int32, (keys, queries), 0)


def load_rows(qkv_ref, nb, half, qs, kt, ks, vs):
    for block in range(nb):
        part = slice(block % 2 * half, block % 2 * half + half)
        at = block // 2
        qs[block] = qkv_ref[at, 0, :, part] * jnp.asarray(HEAD_DIM**-0.5, qs.dtype)
        item = qkv_ref[at, 1, :, part]
        if kt is not None:
            kt[block] = item
        ks[block] = item.T
        if vs is not None:
            vs[block] = qkv_ref[at, 2, :, part].T


def fill_tables(nb, half, seg_ref, order_ref, slot_ref, low_ref, high_ref):
    for block in range(nb):
        slot_ref[order_ref[block]] = jnp.int32(block)
    first = [seg_ref[0, block * half] for block in range(nb)]
    last = [seg_ref[0, block * half + half - 1] for block in range(nb)]
    for block in range(nb):
        if low_ref is not None:
            low_ref[block] = sum(jnp.where(item < first[block], 1, 0) for item in last)
        if high_ref is not None:
            high_ref[block] = sum(jnp.where(item <= last[block], 1, 0) for item in first)


def forward_kernel(half, heads, seg_s, order_ref, seg_ref, qkv_ref, o_ref, full_ref, lse_ref, start_ref, qs, ks, slot_ref, low_ref):
    nb = full_ref.shape[0]

    @pl.when(lax.axis_index("context") < heads)
    def _():
        load_rows(qkv_ref, nb, half, qs, None, ks, None)
        fill_tables(nb, half, seg_s, order_ref, slot_ref, low_ref, None)
        seg = seg_ref[...]
        start = jnp.zeros(seg.shape, jnp.float32)
        for doc in range(1, DOC_LIMIT):
            before = jnp.sum(jnp.where(seg < doc, 1.0, 0.0), axis=1, keepdims=True)
            start = jnp.where(seg == doc, before, start)
        start_ref[...] = start.astype(jnp.int32)

        @pl.loop(0, nb)
        def _(nq):
            slot = slot_ref[nq]
            query = qs[slot]
            begin = start_ref[:, pl.ds(pl.multiple_of(nq * half, 128), half)]
            here = nq * half + lax.broadcasted_iota(jnp.int32, (1, half), 1)

            def step(nk, state):
                top, total, acc = state
                at = slot_ref[nk]
                score = dot(ks[at], query, ((1,), (0,)))
                place = key_positions(nk * half, half, half)
                score = jnp.where((place >= begin) & (place <= here), score, NEG_FILL)
                new_top = jnp.maximum(top, jnp.max(score, axis=0, keepdims=True))
                factor = jnp.exp(top - new_top)
                weight = jnp.exp(score - new_top)
                total = total * factor + jnp.sum(weight, axis=0, keepdims=True)
                value = qkv_ref[at // 2, 2, :, pl.ds(pl.multiple_of(at % 2 * half, 128), half)]
                acc = acc * factor + dot(value, weight.astype(jnp.bfloat16), ((1,), (0,)))
                return new_top, total, acc

            top, total, acc = lax.fori_loop(
                low_ref[nq],
                nq + 1,
                step,
                (
                    jnp.full((1, half), NEG_FILL, jnp.float32),
                    jnp.zeros((1, half), jnp.float32),
                    jnp.zeros((HEAD_DIM, half), jnp.float32),
                ),
            )
            result = acc / total
            full_ref[slot] = result
            lse_ref[slot] = top + jnp.log(total)
            low = result.astype(jnp.bfloat16)
            o_ref[2 * slot] = low[:, : half // 2]
            o_ref[2 * slot + 1] = low[:, half // 2 :]


def attend_forward(qkv, segments, order, half, heads):
    nc = qkv.shape[0]
    nb = 2 * nc
    return pl.pallas_call(
        functools.partial(forward_kernel, half, heads),
        out_shape=(
            jax.ShapeDtypeStruct((2 * nb, HEAD_DIM, half // 2), jnp.bfloat16),
            jax.ShapeDtypeStruct((nb, HEAD_DIM, half), jnp.float32),
            jax.ShapeDtypeStruct((nb, 1, half), jnp.float32),
            jax.ShapeDtypeStruct(segments.shape, jnp.int32),
        ),
        in_specs=[SM, SM, VM, VM],
        out_specs=(VM, VM, VM, VM),
        scratch_shapes=[
            pltpu.VMEM((nb, HEAD_DIM, half), jnp.bfloat16),
            pltpu.VMEM((nb, half, HEAD_DIM), jnp.bfloat16),
            pltpu.SMEM((nb,), jnp.int32),
            pltpu.SMEM((nb,), jnp.int32),
        ],
        compiler_params=pltpu.CompilerParams(vmem_limit_bytes=24 << 20),
    )(segments, order, segments, qkv)


def backward_kernel(
    half, heads, seg_s, order_ref, start_ref, qkv_ref, full_ref, lse_ref, grad_ref, o_ref,
    qs, kt, ks, vs, gs, ds, dq, slot_ref, high_ref,
):
    nb = full_ref.shape[0]

    @pl.when(lax.axis_index("context") < heads)
    def _():
        load_rows(qkv_ref, nb, half, qs, kt, ks, vs)
        fill_tables(nb, half, seg_s, order_ref, slot_ref, None, high_ref)
        for block in range(nb):
            both = jnp.concatenate([grad_ref[2 * block], grad_ref[2 * block + 1]], axis=1)
            gs[block] = both
            ds[block] = jnp.sum(both.astype(jnp.float32) * full_ref[block], axis=0, keepdims=True)
            dq[block] = jnp.zeros((HEAD_DIM, half), jnp.float32)

        @pl.loop(0, nb)
        def _(nk):
            at = slot_ref[nk]
            place = key_positions(nk * half, half, half)

            def step(nq, state):
                grad_key, grad_value = state
                slot = slot_ref[nq]
                query, grad = qs[slot], gs[slot]
                begin = start_ref[:, pl.ds(pl.multiple_of(nq * half, 128), half)]
                here = nq * half + lax.broadcasted_iota(jnp.int32, (1, half), 1)
                score = dot(ks[at], query, ((1,), (0,)))
                score = jnp.where((place >= begin) & (place <= here), score, NEG_FILL)
                weight = jnp.exp(score - lse_ref[slot])
                grad_weight = dot(vs[at], grad, ((1,), (0,)))
                grad_score = (weight * (grad_weight - ds[slot])).astype(jnp.bfloat16)
                grad_value = grad_value + dot(grad, weight.astype(jnp.bfloat16), ((1,), (1,)))
                grad_key = grad_key + dot(query, grad_score, ((1,), (1,)))
                dq[slot] += dot(kt[at], grad_score, ((1,), (0,)))
                return grad_key, grad_value

            zero = jnp.zeros((HEAD_DIM, half), jnp.float32)
            grad_key, grad_value = lax.fori_loop(nk, high_ref[nk], step, (zero, zero))
            columns = pl.ds(pl.multiple_of(at % 2 * half, 128), half)
            o_ref[at // 2, 1, :, columns] = grad_key.astype(jnp.bfloat16)
            o_ref[at // 2, 2, :, columns] = grad_value.astype(jnp.bfloat16)

        for block in range(nb):
            part = slice(block % 2 * half, block % 2 * half + half)
            o_ref[block // 2, 0, :, part] = (dq[block] * HEAD_DIM**-0.5).astype(jnp.bfloat16)


def attend_backward(qkv, segments, order, start, full, lse, grad, half, heads):
    nc = qkv.shape[0]
    nb = 2 * nc
    low = jnp.bfloat16
    return pl.pallas_call(
        functools.partial(backward_kernel, half, heads),
        out_shape=jax.ShapeDtypeStruct(qkv.shape, low),
        in_specs=[SM, SM, VM, VM, VM, VM, VM],
        out_specs=VM,
        scratch_shapes=[
            pltpu.VMEM((nb, HEAD_DIM, half), low),
            pltpu.VMEM((nb, HEAD_DIM, half), low),
            pltpu.VMEM((nb, half, HEAD_DIM), low),
            pltpu.VMEM((nb, half, HEAD_DIM), low),
            pltpu.VMEM((nb, HEAD_DIM, half), low),
            pltpu.VMEM((nb, 1, half), jnp.float32),
            pltpu.VMEM((nb, HEAD_DIM, half), jnp.float32),
            pltpu.SMEM((nb,), jnp.int32),
            pltpu.SMEM((nb,), jnp.int32),
        ],
        compiler_params=pltpu.CompilerParams(vmem_limit_bytes=24 << 20),
    )(segments, order, start, qkv, full, lse, grad)


def norm_parts(values):
    centre = jnp.mean(values, axis=-1, keepdims=True)
    shifted = values - centre
    spread_ = jnp.mean(shifted * shifted, axis=-1, keepdims=True)
    scale = lax.rsqrt(spread_ + NORM_EPS)
    return shifted * scale, scale


def norm_backward(grad, normed, scale, gain):
    e = grad * gain
    mean_e = jnp.mean(e, axis=-1, keepdims=True)
    mean_en = jnp.mean(e * normed, axis=-1, keepdims=True)
    return (e - mean_e - normed * mean_en) * scale


def gelu_tanh(values):
    return jax.nn.gelu(values, approximate=True)


def cross_rows(left, right):
    return lax.dot_general(
        left, right, (((0,), (0,)), ((), ())), preferred_element_type=jnp.float32
    )


def after(value, done):
    return lax.optimization_barrier((value, done))[0]


def per_device(
    mesh_sizes,
    inputs,
    first_gain,
    first_shift,
    project_weight,
    project_bias,
    attend_weight,
    attend_bias,
    second_gain,
    second_shift,
    expand_weight,
    expand_bias,
    shrink_weight,
    shrink_bias,
    segments,
    block_order,
    cotangent,
):
    nt, nc = mesh_sizes["tensor"], mesh_sizes["context"]
    own_rows, width = inputs.shape[1], inputs.shape[2]
    local_width = project_weight.shape[2]
    heads = local_width // HEAD_DIM
    block_rows = own_rows * nt
    half = block_rows // 2
    low = jnp.bfloat16
    f32 = lambda value: value.astype(jnp.float32)
    square = nt == 4 and nc == 4 and mesh_sizes["dp"] == 2
    plane = ("context", "dp")

    tokens_own = f32(inputs[0])
    grad_out = cotangent[0]
    bias = jnp.stack([project_bias[0], jnp.zeros_like(project_bias[0]), project_bias[1]])[:, :, None]
    weight_rows = project_weight.transpose(0, 2, 1)
    if square:
        hidden1_full, attend_full, qkv, grads_near = start_part(
            inputs[0], first_gain, first_shift, attend_weight, weight_rows, bias, grad_out, nt, nc, heads, 0
        )
        pieces, attended_full, lse, start = attend_forward(qkv, segments, block_order, half, heads)
        feed, *feed_pieces, middle, grad_middle, vectors, attend_pieces, grad_heads = feed_part(
            pieces,
            inputs[0],
            attend_full,
            (attend_bias, second_gain, second_shift),
            expand_weight,
            shrink_weight,
            expand_bias,
            grads_near,
            grad_out,
            nt,
            nc,
            heads,
            3,
        )
        grad_qkv = attend_backward(
            qkv, segments, block_order, start, attended_full, lse, grad_heads, half, heads
        )
        outputs, grad_inputs, summed, grad_project, grad_attend, feeds = last_part(
            grad_qkv,
            weight_rows,
            hidden1_full,
            attend_pieces,
            feed,
            middle,
            shrink_bias,
            feed_pieces,
            inputs[0],
            first_gain,
            grad_middle,
            vectors,
            6,
            nt,
            heads,
            7,
        )
        grad_project = grad_project.transpose(0, 2, 1)
        grad_shrink, grad_expand = feeds[0].reshape(-1, width), feeds[1].reshape(width, -1)
        wide = expand_bias.shape[0]
    else:
        hidden1 = norm_parts(tokens_own)[0] * first_gain + first_shift
        hidden1_full = gather_rows(hidden1.astype(low), nt, 0)
        attend_full = lax.all_gather(attend_weight, "tensor", axis=0, tiled=True)
        projected = jnp.einsum(
            "ked,rd->ker", weight_rows, hidden1_full, preferred_element_type=jnp.float32
        )
        projected = (projected + bias).astype(low).reshape(3, heads, HEAD_DIM, block_rows)
        qkv = to_heads(projected, nc, 1)
        pieces, attended_full, lse, start = attend_forward(qkv, segments, block_order, half, heads)
        grad_full = lax.all_gather(grad_out, "tensor", axis=0, tiled=True)
        attended = to_rows(pieces, nc, nt, heads, 2).reshape(width, own_rows)
        middle = tokens_own + cross_rows(attended, attend_full) + attend_bias
        normed2, scale2 = norm_parts(middle)
        hidden2 = (normed2 * second_gain + second_shift).astype(low)
        hidden2_full = gather_rows(hidden2, nt, 3)
        pre_act = jnp.dot(hidden2_full, expand_weight, preferred_element_type=jnp.float32) + expand_bias
        activ = gelu_tanh(pre_act).astype(low)
        grad_act = dot(grad_full, shrink_weight, ((1,), (1,)))
        grad_pre = jax.vjp(gelu_tanh, pre_act)[1](grad_act)[0].astype(low)
        grad_shrink = cross_rows(activ, grad_full).astype(low)
        grad_expand = cross_rows(hidden2_full, grad_pre).astype(low)
        grad_hidden2 = scatter_rows(dot(grad_pre, expand_weight, ((1,), (1,))).astype(low), nt, 4)
        grad_expand_bias = jnp.sum(f32(grad_pre), axis=0)
        feed = jnp.dot(activ, shrink_weight, preferred_element_type=jnp.float32).astype(low)

        grad_shrink_bias = jnp.sum(f32(grad_out), axis=0)
        grad_second_gain = jnp.sum(grad_hidden2 * normed2, axis=0)
        grad_second_shift = jnp.sum(grad_hidden2, axis=0)
        grad_middle = f32(grad_out) + norm_backward(grad_hidden2, normed2, scale2, second_gain)
        grad_middle_low = grad_middle.astype(low)
        grad_attend_bias = jnp.sum(f32(grad_middle_low), axis=0)
        grad_attended = dot(attend_full, grad_middle_low, ((1,), (1,))).astype(low)
        grad_attended = grad_attended.reshape(nt * heads, HEAD_DIM, own_rows)
        grad_attend = jnp.dot(attended, grad_middle_low, preferred_element_type=jnp.float32).astype(low)
        grad_heads = rows_back(grad_attended, nc, nt, heads, 5)
        feed_sum = lax.psum_scatter(after(feed, grad_heads), "tensor", scatter_dimension=0, tiled=True)

        grad_qkv = attend_backward(
            qkv, segments, block_order, start, attended_full, lse, grad_heads, half, heads
        )
        grad_rows = from_heads(grad_qkv, nc, heads, 6).reshape(3 * local_width, block_rows)
        grad_project = dot(hidden1_full, grad_rows, ((0,), (1,))).astype(low)
        grad_hidden1 = cross_rows(grad_rows, weight_rows.reshape(3 * local_width, width)).astype(low)
        row_sums = jnp.sum(f32(grad_rows), axis=1)
        grad_project_bias = jnp.concatenate([row_sums[:local_width], row_sums[2 * local_width :]])
        grad_hidden1 = scatter_rows(grad_hidden1, nt, 7)
        normed1, scale1 = norm_parts(tokens_own)
        back = norm_backward(grad_hidden1, normed1, scale1, first_gain)
        grad_inputs = (grad_middle + back).astype(low)
        wide = grad_expand_bias.shape[0]
        vectors = jnp.concatenate(
            [
                jnp.sum(grad_hidden1 * normed1, axis=0),
                jnp.sum(grad_hidden1, axis=0),
                grad_attend_bias,
                grad_second_gain,
                grad_second_shift,
                grad_shrink_bias,
                grad_expand_bias,
                jnp.pad(grad_project_bias, (0, -(wide + 2 * local_width) % width)),
            ]
        ).reshape(-1, width)
        summed = sum_vectors(vectors, 6, mesh_sizes, 8)
        grad_attend = lax.psum_scatter(grad_attend, "tensor", scatter_dimension=0, tiled=True)
        grad_project, grad_attend, grad_shrink, grad_expand = lax.psum(
            (grad_project, grad_attend, grad_shrink, grad_expand), plane
        )
        grad_project = jnp.stack(
            [grad_project[:, at * local_width : (at + 1) * local_width] for at in range(3)]
        )
        outputs = (middle + f32(feed_sum) + shrink_bias).astype(low)
    tail = summed[6:].reshape(-1)
    return (
        outputs[None],
        grad_inputs[None],
        summed[0],
        summed[1],
        f32(grad_project),
        tail[wide : wide + 2 * local_width].reshape(2, local_width),
        f32(grad_attend),
        summed[2],
        summed[3],
        summed[4],
        f32(grad_expand),
        tail[:wide],
        f32(grad_shrink),
        summed[5],
    )


def solution(mesh):
    rows = P("dp", ("context", "tensor"), None)
    in_specs = (
        rows,
        P(),
        P(),
        P(None, None, "tensor"),
        P(None, "tensor"),
        P("tensor", None),
        P(),
        P(),
        P(),
        P(None, "tensor"),
        P("tensor"),
        P("tensor", None),
        P(),
        P("dp", None),
        P(),
        rows,
    )
    out_specs = (
        rows,
        rows,
        P(),
        P(),
        P(None, None, "tensor"),
        P(None, "tensor"),
        P("tensor", None),
        P(),
        P(),
        P(),
        P(None, "tensor"),
        P("tensor"),
        P("tensor", None),
        P(),
    )
    return jax.shard_map(
        functools.partial(per_device, dict(mesh.shape)),
        mesh=mesh,
        in_specs=in_specs,
        out_specs=out_specs,
        check_vma=False,
    )
```

profile of v0, /device:TPU:0, one launch (start us, length us, event | category | flops | bytes accessed | tf_op | source)
XLA Modules:
  0.0 222.6 jit_solution(11775445330548416034)
XLA Ops:
  0.6 0.8 fusion
  1.4 0.1 pad.1.clone
  1.5 0.1 maximum_bitcast_fusion
  1.6 0.0 copy-start.9
  1.6 0.0 copy-start.18
  1.6 0.2 copy.30.b_hbm
  1.7 0.0 copy-start
  1.7 1.2 copy-done
  2.9 0.0 copy-start.2
  2.9 1.0 copy-done.2
  3.9 0.0 copy-start.4
  3.9 1.0 copy-done.4
  4.8 0.0 copy-start.8
  4.8 1.0 copy-done.8
  5.8 0.0 copy-start.10
  5.8 0.7 copy-done.10
  6.5 0.0 copy-start.12
  6.5 0.7 copy-done.12
  7.2 0.0 copy-start.3
  7.2 0.0 copy-start.5
  7.2 0.0 copy-start.6
  7.2 0.0 copy-start.7
  7.2 0.0 copy-start.14
  7.2 0.0 copy-start.15
  7.2 0.0 copy-start.16
  7.2 0.0 copy-start.17
  7.2 36.0 %shard_map.263 = (bf16[4,192,768]{2,1,0:T(8,128)(2,1)S(1)}, bf16[4,192,768]{2,1,0:T(8,128)(2,1)S(1)}, bf16[4,3,64,768]{3,2,1,0:T(8,128)(2,1)S(1)}, bf16[4,192,768]{2,1,0:T(8,128)(2,1)S(1)}) custom-call(bf16[192,768]{1,0:T(8,128)(2,1)S(1)} %bitcast.21, f32[768]{0:T(1024)S(1)} %copy-done.10, f32[768]{0:T(1024)S(1)} %copy-done.12, ...), custom_call_target="tpu_custom_call" | custom-call | tf_op jit(solution)/shard_map/pallas_call | solution.py:1811
  43.2 0.0 copy-done.9
  43.2 0.0 copy-done.18
  43.2 12.7 %shard_map.264 = (bf16[16,64,192]{2,1,0:T(8,128)(2,1)S(1)}, f32[8,64,384]{2,1,0:T(8,128)S(1)}, f32[8,1,384]{2,1,0:T(1,128)S(1)}, s32[1,3072]{1,0:T(1,128)S(1)}) custom-call(s32[1,3072]{1,0:T(1,128)S(1)} %copy-done.9, s32[8]{0:T(128)S(1)} %copy-done.18, s32[1,3072]{1,0:T(1,128)S(1)} %copy-done.9, bf16[4,3,64,768]{3,2,1,0:T(8,128)(2,1)S(1)} %get-tuple-element.37.qkv_ref), custom_call_target="tpu_custom_call" | custom-call | tf_op jit(solution)/shard_map/pallas_call | solution.py:1929
  56.0 0.0 copy-done.3
  56.0 0.0 copy-done.5
  56.0 0.0 copy-done.6
  56.0 0.0 copy-done.7
  56.0 0.0 copy-done.14
  56.1 0.0 copy-done.15
  56.1 0.0 copy-done.16
  56.1 0.0 copy-done.17
  56.1 84.8 %shard_map.265 = (bf16[768,768]{1,0:T(8,128)(2,1)S(1)}, bf16[2,48,768]{2,1,0:T(8,128)(2,1)S(1)}, bf16[2,48,768]{2,1,0:T(8,128)(2,1)S(1)}, f32[192,768]{1,0:T(8,1...) custom-call(bf16[16,64,192]{2,1,0:T(8,128)(2,1)S(1)} %get-tuple-elem, ...), custom_call_target="tpu_custom_call" | custom-call | tf_op jit(solution)/shard_map/pallas_call | solution.py:1212
  140.9 0.0 copy-start.1
  140.9 0.0 copy-start.11
  140.9 0.0 copy-start.13
  140.9 15.4 %shard_map.266.x_ref = bf16[4,3,64,768]{3,2,1,0:T(8,128)(2,1)S(1)} custom-call(s32[1,3072]{1,0:T(1,128)S(1)} %copy-done.9, s32[8]{0:T(128)S(1)} %copy-done.18, s32[1,3072]{1,0:T(1,128)S(1)} %get-tuple-element.38.start_ref, bf16[4,3,64,768]{3,2,1,0:T(8,128)(2,1)S(1)} %get-tuple-element.37.qkv_ref, f32[8,64,384]{2,1,0:T(8,128)S(1)} %get-tuple-element.39.full_ref, ...), custom_call_target="tpu_custom_call" | custom-call | tf_op jit(solution)/shard_map/pallas_call | solution.py:2001
  156.3 0.0 copy-done.1
  156.3 0.0 copy-done.11
  156.3 0.0 copy-done.13
  156.3 58.6 %shard_map.267 = (bf16[192,768]{1,0:T(8,128)(2,1)S(1)}, bf16[192,768]{1,0:T(8,128)(2,1)S(1)}, f32[8,768]{1,0:T(8,128)S(1)}, bf16[3,192,768]{2,1,0:T(8,128)(2,1)S...) custom-call(bf16[4,3,64,768]{3,2,1,0:T(8,128)(2,1)S(1)} %shard_map.266.x_ref, ...), custom_call_target="tpu_custom_call" | custom-call | tf_op jit(solution)/shard_map/pallas_call | solution.py:1556
  214.9 2.7 %bitcast_convert_fusion = (f32[768,768]{1,0:T(8,128)}, f32[768,768]{1,0:T(8,128)}) fusion(bf16[16,48,768]{2,1,0:T(8,128)(2,1)S(1)} %get-tuple-element.59, bf16[16,48,768]{2,1,0:T(8,128)(2,1)S(1)} %get-tuple-element.58), kind=kLoop, calls=%fused_computation.1 | loop fusion | flops 1179648 | bytes 7077888 | tf_op jit(solution)/shard_map/convert_element_type | solution.py:2076
  217.6 1.3 convert_bitcast_fusion
  219.0 0.9 convert_element_type.23
  219.8 0.7 slice_reduce_fusion
  220.5 0.1 slice.45
  220.6 0.6 slice.53
  221.2 0.7 copy.33
  221.9 0.7 copy.34
  (1 shorter events, 0.0 us)
Async XLA Ops:
  1.6 41.7 %copy-start.9 = (s32[1,3072]{1,0:T(1,128)S(1)}, s32[1,3072]{1,0:T(1,128)}, u32[]{:S(2)}) copy-start(s32[1,3072]{1,0:T(1,128)} %seg_s.3) | copy-start | bytes 36868
  1.6 41.7 %copy-start.18 = (s32[8]{0:T(128)S(1)}, s32[8]{0:T(128)}, u32[]{:S(2)}) copy-start(s32[8]{0:T(128)} %order_ref.3) | copy-start | bytes 100
  1.7 1.2 copy-start
  2.9 1.0 copy-start.2
  3.9 1.0 copy-start.4
  4.8 1.0 copy-start.8
  5.8 0.7 copy-start.10
  6.5 0.7 copy-start.12
  7.2 48.8 %copy-start.3 = (bf16[1,192,768]{2,1,0:T(8,128)(2,1)S(1)}, bf16[1,192,768]{2,1,0:T(8,128)(2,1)}, u32[]{:S(2)}) copy-start(bf16[1,192,768]{2,1,0:T(8,128)(2,1)} %param.16) | copy-start | bytes 884740
  7.2 48.8 %copy-start.5 = (bf16[1,192,768]{2,1,0:T(8,128)(2,1)S(1)}, bf16[1,192,768]{2,1,0:T(8,128)(2,1)}, u32[]{:S(2)}) copy-start(bf16[1,192,768]{2,1,0:T(8,128)(2,1)} %param.31) | copy-start | bytes 884740
  7.2 48.9 %copy-start.6 = (bf16[768,768]{1,0:T(8,128)(2,1)S(1)}, bf16[768,768]{1,0:T(8,128)(2,1)}, u32[]{:S(2)}) copy-start(bf16[768,768]{1,0:T(8,128)(2,1)} %rest_5_.1) | copy-start | bytes 3538948
  7.2 48.9 %copy-start.7 = (bf16[768,768]{1,0:T(8,128)(2,1)S(1)}, bf16[768,768]{1,0:T(8,128)(2,1)}, u32[]{:S(2)}) copy-start(bf16[768,768]{1,0:T(8,128)(2,1)} %rest_6_.1) | copy-start | bytes 3538948
  7.2 48.9 %copy-start.14 = (f32[768]{0:T(1024)S(1)}, f32[768]{0:T(1024)}, u32[]{:S(2)}) copy-start(f32[768]{0:T(1024)} %rest_2_.1) | copy-start | bytes 9220
  7.2 48.9 %copy-start.15 = (f32[768]{0:T(1024)S(1)}, f32[768]{0:T(1024)}, u32[]{:S(2)}) copy-start(f32[768]{0:T(1024)} %rest_3_.2) | copy-start | bytes 9220
  7.2 48.9 %copy-start.16 = (f32[768]{0:T(1024)S(1)}, f32[768]{0:T(1024)}, u32[]{:S(2)}) copy-start(f32[768]{0:T(1024)} %rest_4_.1) | copy-start | bytes 9220
  7.2 48.9 %copy-start.17 = (f32[768]{0:T(1024)S(1)}, f32[768]{0:T(1024)}, u32[]{:S(2)}) copy-start(f32[768]{0:T(1024)} %rest_7_.1) | copy-start | bytes 9220
  140.9 15.4 %copy-start.1 = (bf16[3,768,192]{1,2,0:T(8,128)(2,1)S(1)}, bf16[3,768,192]{1,2,0:T(8,128)(2,1)}, u32[]{:S(2)}) copy-start(bf16[3,768,192]{1,2,0:T(8,128)(2,1)} %param.19) | copy-start | bytes 2654212
  140.9 15.4 %copy-start.11 = (f32[768]{0:T(1024)S(1)}, f32[768]{0:T(1024)}, u32[]{:S(2)}) copy-start(f32[768]{0:T(1024)} %rest_3_.3) | copy-start | bytes 9220
  140.9 15.4 %copy-start.13 = (f32[768]{0:T(1024)S(1)}, f32[768]{0:T(1024)}, u32[]{:S(2)}) copy-start(f32[768]{0:T(1024)} %bias_hbm.1) | copy-start | bytes 9220
where the time goes:
time: 223 us
  Pallas kernels  207 us (93%)
  local copies, waits for them, and re-layouts  9.24 us (4%)
  other arithmetic  4.97 us (2%)
    pallas_call x1, Pallas kernels, feed_part(): pl.pallas_call(functools.partial(feed_kernel, n, nc, heads, chunks), out_...  84.8 us
    pallas_call x1, Pallas kernels, last_part(): pl.pallas_call(functools.partial(last_kernel, n, nc, heads, shared, count...  58.6 us
    pallas_call x1, Pallas kernels, start_part(): pl.pallas_call(functools.partial(start_kernel, n, nc, heads), out_shape=(...  36 us
    pallas_call x1, Pallas kernels, attend_backward(): pl.pallas_call(functools.partial(backward_kernel, half, heads), out_shape...  15.4 us
    pallas_call x1, Pallas kernels, attend_forward(): pl.pallas_call(functools.partial(forward_kernel, half, heads), out_shape=...  12.7 us
    unnamed x40, local copies, waits for them, and re-layouts  6.91 us
    convert_element_type x3, other arithmetic, per_device(): f32 = lambda value: value.astype(jnp.float32)  4.9 us

commit v1 on v0

--- a/solution.py
+++ b/solution.py
@@ -807,11 +807,11 @@
 
 
 def feed_kernel(n, nc, heads, chunks, piece_ref, *rest):
-    (token_hbm, out_ref, abias_hbm, gain_hbm, shift_hbm, up_hbm, down_hbm, bias_hbm, near_ref, cot_ref), rest = rest[:10], rest[10:]
+    (token_hbm, out_hbm, abias_hbm, gain_hbm, shift_hbm, up_hbm, down_hbm, bias_hbm, near_ref, cot_ref), rest = rest[:10], rest[10:]
     outs, heads_ref, rest = rest[:7], rest[7], rest[8:]
     kept_refs, rest = rest[:7], rest[7:]
     feed_ref, p1_ref, p2_ref, middle_ref, gm_ref, vec_ref, p3_ref = kept_refs
-    (token_ref, abias_ref, gain_ref, shift_ref, bias_ref, osem), rest = rest[:6], rest[6:]
+    (token_ref, out_ref, abias_ref, gain_ref, shift_ref, bias_ref, osem), rest = rest[:7], rest[7:]
     leave = copies(tuple(zip(kept_refs, outs)), osem)
     (o_ref, sum_ref, att_ref, gpiece, u3, bsend, brecv, bloc), rest = rest[:8], rest[8:]
     (x_ref, up_ref, down_ref, grad_ref, wsem, asend, arecv, aloc, csend, crecv, cloc), rest = rest[:11], rest[11:]
@@ -838,6 +838,7 @@
             (abias_hbm, abias_ref),
             (gain_hbm, gain_ref),
             (shift_hbm, shift_ref),
+            (out_hbm, out_ref),
             (bias_hbm, bias_ref),
             (up_hbm, up_ref),
             (down_hbm, down_ref),
@@ -853,7 +854,7 @@
     def grad_on(d, s):
         block = jnp.clip(me - s if d == 0 else me + s, 0, n - 1)
         return pltpu.make_async_remote_copy(
-            src_ref=near_ref.at[block] if s == 1 else grad_rows(block),
+            src_ref=near_ref.at[block],
             dst_ref=grad_rows(block),
             send_sem=csend.at[d, s],
             recv_sem=crecv.at[d, s],
@@ -864,29 +865,25 @@
     def grad_sends(d, s):
         return (me - s >= 0) & (me < n - 1) if d == 0 else (me + s < n) & (me > 0)
 
-    def grad_near(d):
-        block = jnp.clip(me - 1 if d == 0 else me + 1, 0, n - 1)
-        return pltpu.make_async_copy(near_ref.at[block], grad_rows(block), cloc.at[d])
+    def grad_near(d, s):
+        block = jnp.clip(me - s if d == 0 else me + s, 0, n - 1)
+        return pltpu.make_async_copy(near_ref.at[block], grad_rows(block), cloc.at[d, s])
 
     def grad_own():
-        return pltpu.make_async_copy(cot_ref, grad_rows(me), cloc.at[2])
-
-    def beside(d):
-        return me > 0 if d == 0 else me < n - 1
+        return pltpu.make_async_copy(cot_ref, grad_rows(me), cloc.at[0, 0])
+
+    def beside(d, s):
+        return me - s >= 0 if d == 0 else me + s < n
 
     grad_own().start()
     for d in range(2):
-
-        @pl.when(beside(d))
-        def _():
-            grad_near(d).start()
+        for s in range(1, n - 1):
+
+            @pl.when(beside(d, s))
+            def _():
+                grad_near(d, s).start()
 
     pl.semaphore_wait(bar, total)
-    for d in range(2):
-
-        @pl.when(grad_sends(d, 1))
-        def _():
-            grad_on(d, 1).start()
 
     def to_place(shift):
         other = lax.rem(place + shift, total)
@@ -907,6 +904,12 @@
         stay.start()
         stay.wait()
 
+    for d in range(2):
+
+        @pl.when(grad_sends(d, n - 2))
+        def _():
+            grad_on(d, n - 2).start()
+
     for shift in range(1, total):
         source = lax.rem(place + total - shift, total)
         at_ctx, at_ten = lax.div(source, n), lax.rem(source, n)
@@ -916,7 +919,7 @@
             landed = att_ref.at[at_ten * heads + jnp.minimum(at_ctx, heads - 1)]
             pltpu.make_async_copy(landed, landed, arecv.at[shift]).wait()
 
-    for item in weights_in[:4]:
+    for item in weights_in[:5]:
         item.wait()
     attended = att_ref[...].reshape(width, rows)
     middle = token_ref[...].astype(f32) + dot(attended, out_ref[...], ((0,), (0,))) + row(abias_ref)
@@ -972,32 +975,16 @@
     own.start()
     sum_ref[...] = jnp.zeros_like(sum_ref)
     own.wait()
-    for item in weights_in[4:]:
+    for item in weights_in[5:]:
         item.wait()
     grad_own().wait()
     for d in range(2):
-
-        @pl.when(beside(d))
-        def _():
-            grad_near(d).wait()
-
-    for s in range(1, n - 1):
-        for d in range(2):
-            block = me - 1 - s if d == 0 else me + 1 + s
-
-            @pl.when((block >= 0) & (block < n))
+        for s in range(1, n - 1):
+
+            @pl.when(beside(d, s))
             def _():
-                landed = grad_rows(jnp.clip(block, 0, n - 1))
-                pltpu.make_async_copy(landed, landed, crecv.at[d, s]).wait()
-
-            if s + 1 < n - 1:
-
-                @pl.when(grad_sends(d, s + 1))
-                def _():
-                    grad_on(d, s + 1).start()
-
-        if s == n - 3:
-            break
+                grad_near(d, s).wait()
+
     columns = 256
 
     def work(block):
@@ -1191,11 +1178,10 @@
                 back(jnp.where(me < block, 0, 1), block, c, True).wait_send()
 
     for d in range(2):
-        for s in range(1, n - 1):
-
-            @pl.when(grad_sends(d, s))
-            def _():
-                grad_on(d, s).wait_send()
+
+        @pl.when(grad_sends(d, n - 2))
+        def _():
+            grad_on(d, n - 2).wait_send()
 
     for item in plane:
         item.reduced()
@@ -1221,7 +1207,7 @@
             jax.ShapeDtypeStruct((2, 2, rows // 4, width // 2), low),
             jax.ShapeDtypeStruct(pieces.shape, low),
         ),
-        in_specs=[VM, HB, VM, HB, HB, HB, HB, HB, HB, VM, HB],
+        in_specs=[VM] + [HB] * 10,
         out_specs=(HB,) * 7 + (VM,),
         scratch_shapes=[
             pltpu.VMEM((total, width), low),
@@ -1232,6 +1218,7 @@
             pltpu.VMEM((8, width), f32),
             pltpu.VMEM((2, 2, rows // 4, width // 2), low),
             pltpu.VMEM(tokens.shape, tokens.dtype),
+            pltpu.VMEM(out_weight.shape, low),
             pltpu.VMEM((width,), f32),
             pltpu.VMEM((width,), f32),
             pltpu.VMEM((width,), f32),
@@ -1249,13 +1236,13 @@
             pltpu.VMEM(up.shape, low),
             pltpu.VMEM(down.shape, low),
             pltpu.VMEM((total, width), low),
-            DMA((7,)),
+            DMA((8,)),
             DMA((nc * n,)),
             DMA((nc * n,)),
             DMA,
             DMA((2, n - 1)),
             DMA((2, n - 1)),
-            DMA((3,)),
+            DMA((2, n - 1)),
             pltpu.VMEM((total, width), low),
             pltpu.VMEM((total, wide), low),
             pltpu.VMEM((total, wide), low),
@@ -1273,7 +1260,7 @@
         ]
         + PlaneSum.reduce_scratch(unit, low) * 2
         + StripSum.reduce_scratch((n, width // n, width), low),
-        compiler_params=remote_params(collective_id, 40),
+        compiler_params=remote_params(collective_id, 56),
     )(pieces, tokens, out_weight, *vectors, up, down, bias, near, cotangent)
 
 
@@ -1372,7 +1359,7 @@
         )
 
     copies_in[0].wait()
-    feed_line.begin((0, 1))
+    feed_line.begin((0,))
     for shift in range(1, n):
         across(shift).start()
     mine = pltpu.make_async_copy(a_hbm.at[lax.div(ten, 2), lax.rem(ten, 2)], land.at[ten], zloc)
@@ -1442,19 +1429,18 @@
     partials(1)
     for line in lines:
         line.begin((2,))
-    feed_line.begin((2,))
+    feed_line.begin((1, 2))
     for item in feeds:
         item.spread2()
     for line in lines:
         line.step(0, first)
-    feed_line.step(1, first)
-    feed_line.step(0, second)
     for kind in range(3):
         grads = rows_ref[kind].reshape(heads * HEAD_DIM, n * own)
         u_ref[kind] = dot(grads, h_ref[...], ((1,), (0,))).astype(low)
     project.begin()
     for line in lines:
         line.step(1, first)
+    feed_line.step(0, second)
     ends = jnp.concatenate(
         [rows_ref[kind].reshape(heads * HEAD_DIM, n * own) for kind in (0, 2)], axis=0
     )
@@ -1467,7 +1453,6 @@
     for k in range(n - 1):
         for line in lines:
             line.step(k, second)
-    feed_line.step(1, second)
     project.third()
     project.spread1()
     for line in lines:
@@ -1515,6 +1500,7 @@
     back = norm_backward(grad, normed, scale, row(gain_ref))
     g_ref[...] = (middle_ref[...] + back).astype(g_ref.dtype)
     project.spread2()
+    feed_line.step(1, first)
     stage_end(0)
     stage_start(1)
     project.spread3()
@@ -1641,6 +1627,11 @@
             def _():
                 self.copy(d, s).start()
 
+    def pass_on(self, d, s, now):
+        @pl.when(self.sends(d, s) & now)
+        def _():
+            self.copy(d, s).start()
+
     def last(self):
         for d in range(2):
             self.wait(d, self.n - 2)
@@ -1683,8 +1674,13 @@
     small = LineGather(n, piece, held, s1, r1)
     large = LineGather(n, x_ref, o_ref, s2, r2)
     grads = LineGather(n, c_ref, g_ref, s5, r5)
+    def move(s):
+        large.step(s)
+        for d in range(2):
+            grads.pass_on(d, 0, me == (s if d == 0 else n - 1 - s))
+
     small.step(0)
-    large.step(0)
+    move(0)
     own = pltpu.make_async_copy(x_ref, o_ref.at[me], loc.at[0])
     own.start()
     mine = pltpu.make_async_copy(piece, held.at[me], loc.at[1])
@@ -1754,14 +1750,13 @@
                 item.start()
 
     near = lax.div(me, 2)
-    large.step(1)
+    move(1)
     weight_in.wait()
     project(near)
     ship_all(0, near)
     hop(1).start()
     for s in range(2, n - 1):
-        large.step(s)
-    grads.step(0)
+        move(s)
     got(0)
     hop(2).start()
     large.last()
@@ -1775,6 +1770,9 @@
     got(1)
     got(2)
     hop(3).start()
+    for d in range(2):
+        grads.wait(d, 0)
+        grads.pass_on(d, 1, me >= 0)
     stay.wait()
 
     @pl.when(ctx < heads)
@@ -1788,11 +1786,11 @@
 
     got(3)
     for d in range(2):
-        grads.wait(d, 0)
+        grads.wait(d, 1)
     result.wait()
     small.finish()
     large.finish()
-    grads.finish(1)
+    grads.finish(2)
     for at in range(4):
         hop(at).wait_send()
     for index in range(2):
@@ -1832,7 +1830,7 @@
         ]
         + [DMA((2, n - 1)) for _ in range(6)]
         + [DMA((4,)), DMA((4,)), DMA((2, nc)), DMA((2, nc)), DMA((6,))],
-        compiler_params=remote_params(collective_id),
+        compiler_params=remote_params(collective_id, 56),
     )(tokens, gain, shift, w, project_weight, bias, cotangent)
     return full.reshape(n * rows, cols), weight.reshape(n * wide, deep), qkv, grads
 

time: 223 us -> 224 us (level)
  local copies, waits for them, and re-layouts: 9.24 us -> 11.5 us
    pallas_call x1, Pallas kernels: 36 us -> 44.1 us  [start_part(): pl.pallas_call(functools.partial(start_kernel, n, nc, heads), out_shape=(...]
    pallas_call x1, Pallas kernels: 84.8 us -> 79.9 us  [feed_part(): pl.pallas_call(functools.partial(feed_kernel, n, nc, heads, chunks), out_...]
    pallas_call x1, Pallas kernels: 58.6 us -> 54.1 us  [last_part(): pl.pallas_call(functools.partial(last_kernel, n, nc, heads, shared, count...]
    unnamed x40 -> x38, local copies, waits for them, and re-layouts: 6.91 us -> 8.5 us
where the time goes in v1:
time: 224 us
  Pallas kernels  206 us (92%)
  local copies, waits for them, and re-layouts  11.5 us (5%)
  other arithmetic  4.97 us (2%)
    pallas_call x1, Pallas kernels, feed_part(): pl.pallas_call(functools.partial(feed_kernel, n, nc, heads, chunks), out_...  79.9 us
    pallas_call x1, Pallas kernels, last_part(): pl.pallas_call(functools.partial(last_kernel, n, nc, heads, shared, count...  54.1 us
    pallas_call x1, Pallas kernels, start_part(): pl.pallas_call(functools.partial(start_kernel, n, nc, heads), out_shape=(...  44.1 us
    pallas_call x1, Pallas kernels, attend_backward(): pl.pallas_call(functools.partial(backward_kernel, half, heads), out_shape...  15.4 us
    pallas_call x1, Pallas kernels, attend_forward(): pl.pallas_call(functools.partial(forward_kernel, half, heads), out_shape=...  12.7 us
    unnamed x38, local copies, waits for them, and re-layouts  8.5 us
    convert_element_type x3, other arithmetic, per_device(): f32 = lambda value: value.astype(jnp.float32)  4.9 us

profile of v1, /device:TPU:0, one launch (start us, length us, event | category | flops | bytes accessed | tf_op | source)
XLA Modules:
  0.0 223.6 jit_solution(4607094858846518595)
XLA Ops:
  0.6 0.8 fusion
  1.4 0.1 pad.1.clone
  1.5 0.1 maximum_bitcast_fusion
  1.6 0.0 copy-start.13
  1.6 0.0 copy-start.17
  1.6 0.9 copy.30.b_hbm
  2.5 44.1 %shard_map.263 = (bf16[4,192,768]{2,1,0:T(8,128)(2,1)}, bf16[4,192,768]{2,1,0:T(8,128)(2,1)}, bf16[4,3,64,768]{3,2,1,0:T(8,128)(2,1)}, bf16[4,192,768]{2,1,0:T(8,128)(2,1)}) custom-call(bf16[192,768]{1,0:T(8,128)(2,1)} %bitcast.21, f32[768]{0:T(1024)} %rest_3_.3, f32[768]{0:T(1024)} %shift_hbm.1, bf16[192,768]{1,0:T(8,128)(2,1)} %full_ref.1, ...), custom_call_target="tpu_custom_call" | custom-call | tf_op jit(solution)/shard_map/pallas_call | solution.py:1809
  46.6 0.0 copy-done.13
  46.6 0.0 copy-done.17
  46.6 0.0 copy-start
  46.6 1.3 copy-done
  47.9 12.7 %shard_map.264 = (bf16[16,64,192]{2,1,0:T(8,128)(2,1)S(1)}, f32[8,64,384]{2,1,0:T(8,128)S(1)}, f32[8,1,384]{2,1,0:T(1,128)S(1)}, s32[1,3072]{1,0:T(1,128)S(1)}) custom-call(s32[1,3072]{1,0:T(1,128)S(1)} %copy-done.13, s32[8]{0:T(128)S(1)} %copy-done.17, s32[1,3072]{1,0:T(1,128)S(1)} %copy-done.13, bf16[4,3,64,768]{3,2,1,0:T(8,128)(2,1)S(1)} %copy-done), custom_call_target="tpu_custom_call" | custom-call | tf_op jit(solution)/shard_map/pallas_call | solution.py:1927
  60.6 0.0 copy-start.9
  60.6 0.8 copy-done.9
  61.4 0.0 copy-start.1
  61.4 79.9 %shard_map.265 = (bf16[768,768]{1,0:T(8,128)(2,1)}, bf16[2,48,768]{2,1,0:T(8,128)(2,1)}, bf16[2,48,768]{2,1,0:T(8,128)(2,1)}, f32[192,768]{1,0:T(8,128)}, f32[19...) custom-call(bf16[16,64,192]{2,1,0:T(8,128)(2,1)} %copy-done.9, ...), custom_call_target="tpu_custom_call" | custom-call | tf_op jit(solution)/shard_map/pallas_call | solution.py:1198
  141.3 0.0 copy-done.1
  141.3 0.0 copy-start.8
  141.4 1.0 copy-done.8
  142.4 0.0 copy-start.2
  142.4 0.0 copy-start.3
  142.4 0.0 copy-start.4
  142.4 0.0 copy-start.5
  142.4 0.0 copy-start.10
  142.4 0.0 copy-start.14
  142.4 0.0 copy-start.15
  142.4 0.0 copy-start.16
  142.4 15.4 %shard_map.266.x_ref = bf16[4,3,64,768]{3,2,1,0:T(8,128)(2,1)S(1)} custom-call(s32[1,3072]{1,0:T(1,128)S(1)} %copy-done.13, s32[8]{0:T(128)S(1)} %copy-done.17, s32[1,3072]{1,0:T(1,128)S(1)} %get-tuple-element.38.start_ref, bf16[4,3,64,768]{3,2,1,0:T(8,128)(2,1)S(1)} %copy-done.1, f32[8,64,384]{2,1,0:T(8,128)S(1)} %get-tuple-element.39.full_ref, ...), custom_call_target="tpu_custom_call" | custom-call | tf_op jit(solution)/shard_map/pallas_call | solution.py:1999
  157.8 0.0 copy-done.2
  157.8 0.0 copy-done.3
  157.9 0.0 copy-done.4
  157.9 0.0 copy-done.5
  157.9 0.0 copy-done.10
  157.9 0.0 copy-done.14
  157.9 0.0 copy-done.15
  157.9 0.0 copy-done.16
  157.9 0.0 copy-start.6
  157.9 1.1 copy-done.6
  159.0 0.0 copy-start.7
  159.0 1.1 copy-done.7
  160.0 0.0 copy-start.11
  160.0 0.9 copy-done.11
  161.0 0.0 copy-start.12
  161.0 0.9 copy-done.12
  161.9 54.1 %shard_map.267 = (bf16[192,768]{1,0:T(8,128)(2,1)S(1)}, bf16[192,768]{1,0:T(8,128)(2,1)S(1)}, f32[8,768]{1,0:T(8,128)S(1)}, bf16[3,192,768]{2,1,0:T(8,128)(2,1)S...) custom-call(bf16[4,3,64,768]{3,2,1,0:T(8,128)(2,1)S(1)} %shard_map.266.x_ref, ...), custom_call_target="tpu_custom_call" | custom-call | tf_op jit(solution)/shard_map/pallas_call | solution.py:1542
  215.9 2.7 %bitcast_convert_fusion = (f32[768,768]{1,0:T(8,128)}, f32[768,768]{1,0:T(8,128)}) fusion(bf16[16,48,768]{2,1,0:T(8,128)(2,1)S(1)} %get-tuple-element.59, bf16[16,48,768]{2,1,0:T(8,128)(2,1)S(1)} %get-tuple-element.58), kind=kLoop, calls=%fused_computation.1 | loop fusion | flops 1179648 | bytes 7077888 | tf_op jit(solution)/shard_map/convert_element_type | solution.py:2074
  218.6 1.3 convert_bitcast_fusion
  220.0 0.9 convert_element_type.23
  220.8 0.7 slice_reduce_fusion
  221.5 0.1 slice.45
  221.6 0.6 slice.53
  222.2 0.7 copy.33
  222.9 0.7 copy.34
  (1 shorter events, 0.0 us)
Async XLA Ops:
  1.6 45.0 %copy-start.13 = (s32[1,3072]{1,0:T(1,128)S(1)}, s32[1,3072]{1,0:T(1,128)}, u32[]{:S(2)}) copy-start(s32[1,3072]{1,0:T(1,128)} %seg_s.3) | copy-start | bytes 36868
  1.6 45.0 %copy-start.17 = (s32[8]{0:T(128)S(1)}, s32[8]{0:T(128)}, u32[]{:S(2)}) copy-start(s32[8]{0:T(128)} %order_ref.3) | copy-start | bytes 100
  46.6 1.3 copy-start
  60.6 0.8 copy-start.9
  61.4 79.9 %copy-start.1 = (bf16[4,3,64,768]{3,2,1,0:T(8,128)(2,1)S(1)}, bf16[4,3,64,768]{3,2,1,0:T(8,128)(2,1)}, u32[]{:S(2)}) copy-start(bf16[4,3,64,768]{3,2,1,0:T(8,128)(2,1)} %get-tuple-element.37.qkv_ref) | copy-start | bytes 3538948
  141.3 1.0 copy-start.8
  142.4 15.4 %copy-start.2 = (bf16[3,768,192]{1,2,0:T(8,128)(2,1)S(1)}, bf16[3,768,192]{1,2,0:T(8,128)(2,1)}, u32[]{:S(2)}) copy-start(bf16[3,768,192]{1,2,0:T(8,128)(2,1)} %param.19) | copy-start | bytes 2654212
  142.4 15.5 %copy-start.3 = (bf16[1,192,768]{2,1,0:T(8,128)(2,1)S(1)}, bf16[1,192,768]{2,1,0:T(8,128)(2,1)}, u32[]{:S(2)}) copy-start(bf16[1,192,768]{2,1,0:T(8,128)(2,1)} %param.16) | copy-start | bytes 884740
  142.4 15.5 %copy-start.4 = (bf16[4,192,768]{2,1,0:T(8,128)(2,1)S(1)}, bf16[4,192,768]{2,1,0:T(8,128)(2,1)}, u32[]{:S(2)}) copy-start(bf16[4,192,768]{2,1,0:T(8,128)(2,1)} %get-tuple-element.45) | copy-start | bytes 3538948
  142.4 15.5 %copy-start.5 = (bf16[768,768]{1,0:T(8,128)(2,1)S(1)}, bf16[768,768]{1,0:T(8,128)(2,1)}, u32[]{:S(2)}) copy-start(bf16[768,768]{1,0:T(8,128)(2,1)} %get-tuple-element.47) | copy-start | bytes 3538948
  142.4 15.5 %copy-start.10 = (bf16[2,48,768]{2,1,0:T(8,128)(2,1)S(1)}, bf16[2,48,768]{2,1,0:T(8,128)(2,1)}, u32[]{:S(2)}) copy-start(bf16[2,48,768]{2,1,0:T(8,128)(2,1)} %get-tuple-element.49.rest_0_) | copy-start | bytes 442372
  142.4 15.5 %copy-start.14 = (f32[8,768]{1,0:T(8,128)S(1)}, f32[8,768]{1,0:T(8,128)}, u32[]{:S(2)}) copy-start(f32[8,768]{1,0:T(8,128)} %get-tuple-element.52.rest_5_) | copy-start | bytes 73732
  142.4 15.5 %copy-start.15 = (f32[768]{0:T(1024)S(1)}, f32[768]{0:T(1024)}, u32[]{:S(2)}) copy-start(f32[768]{0:T(1024)} %rest_3_.3) | copy-start | bytes 9220
  142.4 15.5 %copy-start.16 = (f32[768]{0:T(1024)S(1)}, f32[768]{0:T(1024)}, u32[]{:S(2)}) copy-start(f32[768]{0:T(1024)} %bias_hbm.1) | copy-start | bytes 9220
  157.9 1.1 copy-start.6
  159.0 1.1 copy-start.7
  160.0 0.9 copy-start.11
  161.0 0.9 copy-start.12

commit v2 on v0

--- a/solution.py
+++ b/solution.py
@@ -882,11 +882,6 @@
             grad_near(d).start()
 
     pl.semaphore_wait(bar, total)
-    for d in range(2):
-
-        @pl.when(grad_sends(d, 1))
-        def _():
-            grad_on(d, 1).start()
 
     def to_place(shift):
         other = lax.rem(place + shift, total)
@@ -906,6 +901,12 @@
         stay = pltpu.make_async_copy(piece_ref.at[place], att_ref.at[my_head], aloc)
         stay.start()
         stay.wait()
+
+    for d in range(2):
+
+        @pl.when(grad_sends(d, 1))
+        def _():
+            grad_on(d, 1).start()
 
     for shift in range(1, total):
         source = lax.rem(place + total - shift, total)
@@ -1372,7 +1373,7 @@
         )
 
     copies_in[0].wait()
-    feed_line.begin((0, 1))
+    feed_line.begin((0,))
     for shift in range(1, n):
         across(shift).start()
     mine = pltpu.make_async_copy(a_hbm.at[lax.div(ten, 2), lax.rem(ten, 2)], land.at[ten], zloc)
@@ -1442,19 +1443,18 @@
     partials(1)
     for line in lines:
         line.begin((2,))
-    feed_line.begin((2,))
+    feed_line.begin((1, 2))
     for item in feeds:
         item.spread2()
     for line in lines:
         line.step(0, first)
-    feed_line.step(1, first)
-    feed_line.step(0, second)
     for kind in range(3):
         grads = rows_ref[kind].reshape(heads * HEAD_DIM, n * own)
         u_ref[kind] = dot(grads, h_ref[...], ((1,), (0,))).astype(low)
     project.begin()
     for line in lines:
         line.step(1, first)
+    feed_line.step(0, second)
     ends = jnp.concatenate(
         [rows_ref[kind].reshape(heads * HEAD_DIM, n * own) for kind in (0, 2)], axis=0
     )
@@ -1467,7 +1467,6 @@
     for k in range(n - 1):
         for line in lines:
             line.step(k, second)
-    feed_line.step(1, second)
     project.third()
     project.spread1()
     for line in lines:
@@ -1515,6 +1514,7 @@
     back = norm_backward(grad, normed, scale, row(gain_ref))
     g_ref[...] = (middle_ref[...] + back).astype(g_ref.dtype)
     project.spread2()
+    feed_line.step(1, first)
     stage_end(0)
     stage_start(1)
     project.spread3()
@@ -1641,6 +1641,11 @@
             def _():
                 self.copy(d, s).start()
 
+    def pass_on(self, d, s, now):
+        @pl.when(self.sends(d, s) & now)
+        def _():
+            self.copy(d, s).start()
+
     def last(self):
         for d in range(2):
             self.wait(d, self.n - 2)
@@ -1683,8 +1688,13 @@
     small = LineGather(n, piece, held, s1, r1)
     large = LineGather(n, x_ref, o_ref, s2, r2)
     grads = LineGather(n, c_ref, g_ref, s5, r5)
+    def move(s):
+        large.step(s)
+        for d in range(2):
+            grads.pass_on(d, 0, me == (s if d == 0 else n - 1 - s))
+
     small.step(0)
-    large.step(0)
+    move(0)
     own = pltpu.make_async_copy(x_ref, o_ref.at[me], loc.at[0])
     own.start()
     mine = pltpu.make_async_copy(piece, held.at[me], loc.at[1])
@@ -1754,14 +1764,13 @@
                 item.start()
 
     near = lax.div(me, 2)
-    large.step(1)
+    move(1)
     weight_in.wait()
     project(near)
     ship_all(0, near)
     hop(1).start()
     for s in range(2, n - 1):
-        large.step(s)
-    grads.step(0)
+        move(s)
     got(0)
     hop(2).start()
     large.last()
@@ -1832,7 +1841,7 @@
         ]
         + [DMA((2, n - 1)) for _ in range(6)]
         + [DMA((4,)), DMA((4,)), DMA((2, nc)), DMA((2, nc)), DMA((6,))],
-        compiler_params=remote_params(collective_id),
+        compiler_params=remote_params(collective_id, 56),
     )(tokens, gain, shift, w, project_weight, bias, cotangent)
     return full.reshape(n * rows, cols), weight.reshape(n * wide, deep), qkv, grads
 

time: 223 us -> 218 us (0.978)
  Pallas kernels: 207 us -> 204 us
    pallas_call x1, Pallas kernels: 58.6 us -> 54.2 us  [last_part(): pl.pallas_call(functools.partial(last_kernel, n, nc, heads, shared, count...]
    pallas_call x1, Pallas kernels: 84.8 us -> 81 us  [feed_part(): pl.pallas_call(functools.partial(feed_kernel, n, nc, heads, chunks), out_...]
    pallas_call x1, Pallas kernels: 36 us -> 39.3 us  [start_part(): pl.pallas_call(functools.partial(start_kernel, n, nc, heads), out_shape=(...]
    unnamed x40 -> x38, local copies, waits for them, and re-layouts: 6.91 us -> 5.3 us
where the time goes in v2:
time: 218 us
  Pallas kernels  204 us (94%)
  local copies, waits for them, and re-layouts  8.34 us (4%)
  other arithmetic  4.97 us (2%)
    pallas_call x1, Pallas kernels, feed_part(): pl.pallas_call(functools.partial(feed_kernel, n, nc, heads, chunks), out_...  81 us
    pallas_call x1, Pallas kernels, last_part(): pl.pallas_call(functools.partial(last_kernel, n, nc, heads, shared, count...  54.2 us
    pallas_call x1, Pallas kernels, start_part(): pl.pallas_call(functools.partial(start_kernel, n, nc, heads), out_shape=(...  39.3 us
    pallas_call x1, Pallas kernels, attend_backward(): pl.pallas_call(functools.partial(backward_kernel, half, heads), out_shape...  16 us
    pallas_call x1, Pallas kernels, attend_forward(): pl.pallas_call(functools.partial(forward_kernel, half, heads), out_shape=...  13.2 us
    unnamed x38, local copies, waits for them, and re-layouts  5.3 us
    convert_element_type x3, other arithmetic, per_device(): f32 = lambda value: value.astype(jnp.float32)  4.9 us

profile of v2, /device:TPU:0, one launch (start us, length us, event | category | flops | bytes accessed | tf_op | source)
XLA Modules:
  0.0 218.1 jit_solution(6646401883795238116)
XLA Ops:
  0.6 0.8 fusion
  1.4 0.1 pad.1.clone
  1.5 0.1 maximum_bitcast_fusion
  1.6 0.0 copy-start.10
  1.6 0.0 copy-start.17
  1.6 0.9 copy.30.b_hbm
  2.4 0.0 copy-start.3
  2.5 0.0 copy-start.4
  2.5 0.0 copy-start.5
  2.5 0.0 copy-start.13
  2.5 0.0 copy-start.14
  2.5 0.0 copy-start.15
  2.5 0.0 copy-start.16
  2.5 39.3 %shard_map.263 = (bf16[4,192,768]{2,1,0:T(8,128)(2,1)}, bf16[4,192,768]{2,1,0:T(8,128)(2,1)}, bf16[4,3,64,768]{3,2,1,0:T(8,128)(2,1)}, bf16[4,192,768]{2,1,0:T(8,128)(2,1)}) custom-call(bf16[192,768]{1,0:T(8,128)(2,1)} %bitcast.21, f32[768]{0:T(1024)} %rest_3_.3, f32[768]{0:T(1024)} %shift_hbm.1, bf16[192,768]{1,0:T(8,128)(2,1)} %full_ref.1, ...), custom_call_target="tpu_custom_call" | custom-call | tf_op jit(solution)/shard_map/pallas_call | solution.py:1820
  41.8 0.0 copy-done.10
  41.9 0.0 copy-done.17
  41.9 0.0 copy-start
  41.9 1.3 copy-done
  43.1 0.0 copy-start.6
  43.1 13.2 %shard_map.264 = (bf16[16,64,192]{2,1,0:T(8,128)(2,1)S(1)}, f32[8,64,384]{2,1,0:T(8,128)S(1)}, f32[8,1,384]{2,1,0:T(1,128)S(1)}, s32[1,3072]{1,0:T(1,128)S(1)}) custom-call(s32[1,3072]{1,0:T(1,128)S(1)} %copy-done.10, s32[8]{0:T(128)S(1)} %copy-done.17, s32[1,3072]{1,0:T(1,128)S(1)} %copy-done.10, bf16[4,3,64,768]{3,2,1,0:T(8,128)(2,1)S(1)} %copy-done), custom_call_target="tpu_custom_call" | custom-call | tf_op jit(solution)/shard_map/pallas_call | solution.py:1938
  56.4 0.0 copy-done.3
  56.4 0.0 copy-done.4
  56.4 0.0 copy-done.5
  56.4 0.0 copy-done.13
  56.4 0.0 copy-done.14
  56.4 0.0 copy-done.15
  56.5 0.0 copy-done.16
  56.5 0.0 copy-done.6
  56.5 0.0 copy-start.8
  56.5 1.3 copy-done.8
  57.7 0.0 copy-start.9
  57.7 1.3 copy-done.9
  59.0 0.0 copy-start.1
  59.0 81.0 %shard_map.265 = (bf16[768,768]{1,0:T(8,128)(2,1)S(1)}, bf16[2,48,768]{2,1,0:T(8,128)(2,1)S(1)}, bf16[2,48,768]{2,1,0:T(8,128)(2,1)S(1)}, f32[192,768]{1,0:T(8,1...) custom-call(bf16[16,64,192]{2,1,0:T(8,128)(2,1)S(1)} %get-tuple-elem, ...), custom_call_target="tpu_custom_call" | custom-call | tf_op jit(solution)/shard_map/pallas_call | solution.py:1213
  140.1 0.0 copy-done.1
  140.1 0.0 copy-start.2
  140.1 0.0 copy-start.7
  140.1 0.0 copy-start.11
  140.1 0.0 copy-start.12
  140.1 16.0 %shard_map.266.x_ref = bf16[4,3,64,768]{3,2,1,0:T(8,128)(2,1)S(1)} custom-call(s32[1,3072]{1,0:T(1,128)S(1)} %copy-done.10, s32[8]{0:T(128)S(1)} %copy-done.17, s32[1,3072]{1,0:T(1,128)S(1)} %get-tuple-element.38.start_ref, bf16[4,3,64,768]{3,2,1,0:T(8,128)(2,1)S(1)} %copy-done.1, f32[8,64,384]{2,1,0:T(8,128)S(1)} %get-tuple-element.39.full_ref, ...), custom_call_target="tpu_custom_call" | custom-call | tf_op jit(solution)/shard_map/pallas_call | solution.py:2010
  156.2 0.0 copy-done.2
  156.2 0.0 copy-done.7
  156.2 0.0 copy-done.11
  156.2 0.0 copy-done.12
  156.2 54.2 %shard_map.267 = (bf16[192,768]{1,0:T(8,128)(2,1)S(1)}, bf16[192,768]{1,0:T(8,128)(2,1)S(1)}, f32[8,768]{1,0:T(8,128)S(1)}, bf16[3,192,768]{2,1,0:T(8,128)(2,1)S...) custom-call(bf16[4,3,64,768]{3,2,1,0:T(8,128)(2,1)S(1)} %shard_map.266.x_ref, ...), custom_call_target="tpu_custom_call" | custom-call | tf_op jit(solution)/shard_map/pallas_call | solution.py:1556
  210.4 2.7 %bitcast_convert_fusion = (f32[768,768]{1,0:T(8,128)}, f32[768,768]{1,0:T(8,128)}) fusion(bf16[16,48,768]{2,1,0:T(8,128)(2,1)S(1)} %get-tuple-element.59, bf16[16,48,768]{2,1,0:T(8,128)(2,1)S(1)} %get-tuple-element.58), kind=kLoop, calls=%fused_computation.1 | loop fusion | flops 1179648 | bytes 7077888 | tf_op jit(solution)/shard_map/convert_element_type | solution.py:2085
  213.1 1.3 convert_bitcast_fusion
  214.5 0.9 convert_element_type.23
  215.3 0.7 slice_reduce_fusion
  216.0 0.1 slice.45
  216.1 0.6 slice.53
  216.7 0.7 copy.33
  217.4 0.7 copy.34
  (1 shorter events, 0.0 us)
Async XLA Ops:
  1.6 40.3 %copy-start.10 = (s32[1,3072]{1,0:T(1,128)S(1)}, s32[1,3072]{1,0:T(1,128)}, u32[]{:S(2)}) copy-start(s32[1,3072]{1,0:T(1,128)} %seg_s.3) | copy-start | bytes 36868
  1.6 40.3 %copy-start.17 = (s32[8]{0:T(128)S(1)}, s32[8]{0:T(128)}, u32[]{:S(2)}) copy-start(s32[8]{0:T(128)} %order_ref.3) | copy-start | bytes 100
  2.4 53.9 %copy-start.3 = (bf16[1,192,768]{2,1,0:T(8,128)(2,1)S(1)}, bf16[1,192,768]{2,1,0:T(8,128)(2,1)}, u32[]{:S(2)}) copy-start(bf16[1,192,768]{2,1,0:T(8,128)(2,1)} %param.16) | copy-start | bytes 884740
  2.5 54.0 %copy-start.4 = (bf16[1,192,768]{2,1,0:T(8,128)(2,1)S(1)}, bf16[1,192,768]{2,1,0:T(8,128)(2,1)}, u32[]{:S(2)}) copy-start(bf16[1,192,768]{2,1,0:T(8,128)(2,1)} %param.31) | copy-start | bytes 884740
  2.5 54.0 %copy-start.5 = (bf16[768,768]{1,0:T(8,128)(2,1)S(1)}, bf16[768,768]{1,0:T(8,128)(2,1)}, u32[]{:S(2)}) copy-start(bf16[768,768]{1,0:T(8,128)(2,1)} %rest_5_.1) | copy-start | bytes 3538948
  2.5 54.0 %copy-start.13 = (f32[768]{0:T(1024)S(1)}, f32[768]{0:T(1024)}, u32[]{:S(2)}) copy-start(f32[768]{0:T(1024)} %rest_2_.1) | copy-start | bytes 9220
  2.5 54.0 %copy-start.14 = (f32[768]{0:T(1024)S(1)}, f32[768]{0:T(1024)}, u32[]{:S(2)}) copy-start(f32[768]{0:T(1024)} %rest_3_.2) | copy-start | bytes 9220
  2.5 54.0 %copy-start.15 = (f32[768]{0:T(1024)S(1)}, f32[768]{0:T(1024)}, u32[]{:S(2)}) copy-start(f32[768]{0:T(1024)} %rest_4_.1) | copy-start | bytes 9220
  2.5 54.0 %copy-start.16 = (f32[768]{0:T(1024)S(1)}, f32[768]{0:T(1024)}, u32[]{:S(2)}) copy-start(f32[768]{0:T(1024)} %rest_7_.1) | copy-start | bytes 9220
  41.9 1.3 copy-start
  43.1 13.3 %copy-start.6 = (bf16[768,768]{1,0:T(8,128)(2,1)S(1)}, bf16[768,768]{1,0:T(8,128)(2,1)}, u32[]{:S(2)}) copy-start(bf16[768,768]{1,0:T(8,128)(2,1)} %rest_6_.1) | copy-start | bytes 3538948
  56.5 1.3 copy-start.8
  57.7 1.3 copy-start.9
  59.0 81.0 %copy-start.1 = (bf16[4,3,64,768]{3,2,1,0:T(8,128)(2,1)S(1)}, bf16[4,3,64,768]{3,2,1,0:T(8,128)(2,1)}, u32[]{:S(2)}) copy-start(bf16[4,3,64,768]{3,2,1,0:T(8,128)(2,1)} %get-tuple-element.37.qkv_ref) | copy-start | bytes 3538948
  140.1 16.1 %copy-start.2 = (bf16[3,768,192]{1,2,0:T(8,128)(2,1)S(1)}, bf16[3,768,192]{1,2,0:T(8,128)(2,1)}, u32[]{:S(2)}) copy-start(bf16[3,768,192]{1,2,0:T(8,128)(2,1)} %param.19) | copy-start | bytes 2654212
  140.1 16.1 %copy-start.7 = (bf16[4,192,768]{2,1,0:T(8,128)(2,1)S(1)}, bf16[4,192,768]{2,1,0:T(8,128)(2,1)}, u32[]{:S(2)}) copy-start(bf16[4,192,768]{2,1,0:T(8,128)(2,1)} %get-tuple-element.45) | copy-start | bytes 3538948
  140.1 16.1 %copy-start.11 = (f32[768]{0:T(1024)S(1)}, f32[768]{0:T(1024)}, u32[]{:S(2)}) copy-start(f32[768]{0:T(1024)} %rest_3_.3) | copy-start | bytes 9220
  140.1 16.1 %copy-start.12 = (f32[768]{0:T(1024)S(1)}, f32[768]{0:T(1024)}, u32[]{:S(2)}) copy-start(f32[768]{0:T(1024)} %bias_hbm.1) | copy-start | bytes 9220

commit v3 on v2

--- a/solution.py
+++ b/solution.py
@@ -810,15 +810,14 @@
     (token_hbm, out_ref, abias_hbm, gain_hbm, shift_hbm, up_hbm, down_hbm, bias_hbm, near_ref, cot_ref), rest = rest[:10], rest[10:]
     outs, heads_ref, rest = rest[:7], rest[7], rest[8:]
     kept_refs, rest = rest[:7], rest[7:]
-    feed_ref, p1_ref, p2_ref, middle_ref, gm_ref, vec_ref, p3_ref = kept_refs
+    feed_ref, p1_ref, p2_ref, middle_ref, gm_ref, vec_ref, u3 = kept_refs
     (token_ref, abias_ref, gain_ref, shift_ref, bias_ref, osem), rest = rest[:6], rest[6:]
     leave = copies(tuple(zip(kept_refs, outs)), osem)
-    (o_ref, sum_ref, att_ref, gpiece, u3, bsend, brecv, bloc), rest = rest[:8], rest[8:]
+    (o_ref, sum_ref, att_ref, gpiece, bsend, brecv, bloc), rest = rest[:7], rest[7:]
     (x_ref, up_ref, down_ref, grad_ref, wsem, asend, arecv, aloc, csend, crecv, cloc), rest = rest[:11], rest[11:]
     (held, act, gp, part, acc, buf, tmp, u1, u2), rest = rest[:9], rest[9:]
     (gsend, grecv, loc, ssend, srecv), rest = rest[:5], rest[5:]
     plane = [PlaneSum(u1, p1_ref, None, rest[:10]), PlaneSum(u2, p2_ref, None, rest[10:20])]
-    out_sum = StripSum(u3, p3_ref, None, rest[20:30])
     me = lax.axis_index("tensor")
     rows, width = token_ref.shape
     wide = up_ref.shape[1]
@@ -1147,16 +1146,12 @@
     stay = pltpu.make_async_copy(gpiece.at[my_head], heads_ref.at[place], bloc)
     stay.start()
     u3[...] = dot(att_ref[...].reshape(width, rows), gm_low, ((1,), (0,))).astype(low).reshape(u3.shape)
-    out_sum.begin()
+    leave[6].start()
     vec_ref[3:4, :] = jnp.sum(grad * normed, axis=0, keepdims=True)
     vec_ref[4:5, :] = jnp.sum(grad, axis=0, keepdims=True)
     vec_ref[5:6, :] = jnp.sum(above, axis=0, keepdims=True)
     vec_ref[6:7, :] = sum_ref[...]
-    out_sum.first()
-    out_sum.second()
-    out_sum.third()
     leave[5].start()
-    leave[6].start()
     stay.wait()
 
     @pl.when(ctx < heads)
@@ -1173,7 +1168,6 @@
         def _():
             item.wait_send()
 
-    out_sum.reduced()
     for item in leave:
         item.wait()
     for d in range(2):
@@ -1205,7 +1199,7 @@
 def feed_part(pieces, tokens, out_weight, vectors, up, down, bias, near, cotangent, n, nc, heads, collective_id):
     rows, width = tokens.shape
     wide = up.shape[1]
-    chunks = 2
+    chunks = 4
     total = n * rows
     low, f32 = jnp.bfloat16, jnp.float32
     unit = (16, wide // 16, width)
@@ -1219,7 +1213,7 @@
             jax.ShapeDtypeStruct((rows, width), f32),
             jax.ShapeDtypeStruct((rows, width), f32),
             jax.ShapeDtypeStruct((8, width), f32),
-            jax.ShapeDtypeStruct((2, 2, rows // 4, width // 2), low),
+            jax.ShapeDtypeStruct((n, width // n, width), low),
             jax.ShapeDtypeStruct(pieces.shape, low),
         ),
         in_specs=[VM, HB, VM, HB, HB, HB, HB, HB, HB, VM, HB],
@@ -1231,7 +1225,7 @@
             pltpu.VMEM((rows, width), f32),
             pltpu.VMEM((rows, width), f32),
             pltpu.VMEM((8, width), f32),
-            pltpu.VMEM((2, 2, rows // 4, width // 2), low),
+            pltpu.VMEM((n, width // n, width), low),
             pltpu.VMEM(tokens.shape, tokens.dtype),
             pltpu.VMEM((width,), f32),
             pltpu.VMEM((width,), f32),
@@ -1242,7 +1236,6 @@
             pltpu.VMEM((1, wide), f32),
             pltpu.VMEM((n * heads,) + pieces.shape[1:], low),
             pltpu.VMEM((n * heads,) + pieces.shape[1:], low),
-            pltpu.VMEM((n, width // n, width), low),
             DMA((nc * n,)),
             DMA((nc * n,)),
             DMA,
@@ -1272,8 +1265,8 @@
             DMA((n, chunks)),
             DMA((2, n, chunks)),
         ]
-        + PlaneSum.reduce_scratch(unit, low) * 2
-        + StripSum.reduce_scratch((n, width // n, width), low),
+        + PlaneSum.reduce_scratch(unit, low) * 2,
+
         compiler_params=remote_params(collective_id, 40),
     )(pieces, tokens, out_weight, *vectors, up, down, bias, near, cotangent)
 
@@ -1288,7 +1281,7 @@
     (feed_ref, fsum_ref, mid_ref, bias_ref, gain_ref, vec_ref), rest = rest[:6], rest[6:]
     feed_line = LineScatter(n, feed_ref, fsum_ref, *rest[:4])
     rest = rest[4:]
-    chunks = 2
+    chunks = 4
     own = token_ref.shape[0]
     few = own // chunks
     lines = [
@@ -1300,7 +1293,9 @@
     rest = rest[13:]
     feeds = [PlaneSum(None, ps[i], outs[i], None, rest[3 * i : 3 * i + 3]) for i in range(count)]
     rest = rest[3 * count :]
-    (land, zsend, zrecv, zloc, a_ref), rest = rest[:5], rest[5:]
+    (land, zsend, zrecv, zloc, a_ref, strip_ref, strip_piece), rest = rest[:7], rest[7:]
+    attend = StripSum(strip_ref, strip_piece, None, rest[:10])
+    rest = rest[10:]
     (asend, arecv, aloc, now), rest = rest[:4], rest[4:]
     sizes = (n, 2 * nc)
     bufs, sems = rest[:2], rest[2:]
@@ -1319,6 +1314,7 @@
     copies_in = copies(
         (
             (feed_hbm, feed_ref),
+            (a_hbm, strip_ref),
             (token_hbm, token_ref),
             (w_hbm, w_ref),
             (h_hbm, h_ref),
@@ -1364,7 +1360,7 @@
     def across(shift):
         other = lax.rem(ten + shift, n)
         return pltpu.make_async_remote_copy(
-            src_ref=a_hbm.at[lax.div(other, 2), lax.rem(other, 2)],
+            src_ref=strip_piece.at[lax.div(other, 2), lax.rem(other, 2)],
             dst_ref=land.at[ten],
             send_sem=zsend.at[shift],
             recv_sem=zrecv.at[shift],
@@ -1374,10 +1370,9 @@
 
     copies_in[0].wait()
     feed_line.begin((0,))
-    for shift in range(1, n):
-        across(shift).start()
-    mine = pltpu.make_async_copy(a_hbm.at[lax.div(ten, 2), lax.rem(ten, 2)], land.at[ten], zloc)
-    mine.start()
+    mine = pltpu.make_async_copy(strip_piece.at[lax.div(ten, 2), lax.rem(ten, 2)], land.at[ten], zloc)
+    copies_in[1].wait()
+    attend.begin()
     for item in feeds:
         item.spread1()
 
@@ -1400,23 +1395,31 @@
             device_id_type=MESH,
         )
 
-    copies_in[1].wait()
-    normed, scale = norm_parts(token_ref[...].astype(f32))
-    mine.wait()
-    for shift in range(1, n):
-        source = lax.rem(ten + n - shift, n)
-        pltpu.make_async_copy(land.at[source], land.at[source], zrecv.at[shift]).wait()
-    value = land[0].astype(f32)
-    for at in range(1, n):
-        value = value + land[at].astype(f32)
-    a_ref[...] = value.astype(low)
+    kept = pltpu.make_async_copy(a_ref, there(place), aloc)
+
+    def exchange():
+        for shift in range(1, n):
+            across(shift).start()
+        mine.start()
+
+    def gathered():
+        mine.wait()
+        for shift in range(1, n):
+            source = lax.rem(ten + n - shift, n)
+            pltpu.make_async_copy(land.at[source], land.at[source], zrecv.at[shift]).wait()
+        value = land[0].astype(f32)
+        for at in range(1, n):
+            value = value + land[at].astype(f32)
+        a_ref[...] = value.astype(low)
+        for shift in range(1, 8):
+            push(shift).start()
+        kept.start()
+
     for item in copies_in[2:]:
         item.wait()
+    normed, scale = norm_parts(token_ref[...].astype(f32))
     now[0] = vec_ref[...]
-    for shift in range(1, 8):
-        push(shift).start()
-    kept = pltpu.make_async_copy(a_ref, there(place), aloc)
-    kept.start()
+    attend.first()
 
     def partials(index):
         at = columns(pairs[index])
@@ -1443,11 +1446,14 @@
     partials(1)
     for line in lines:
         line.begin((2,))
-    feed_line.begin((1, 2))
     for item in feeds:
         item.spread2()
+    attend.second()
     for line in lines:
         line.step(0, first)
+    attend.third()
+    exchange()
+    feed_line.begin((1, 2))
     for kind in range(3):
         grads = rows_ref[kind].reshape(heads * HEAD_DIM, n * own)
         u_ref[kind] = dot(grads, h_ref[...], ((1,), (0,))).astype(low)
@@ -1460,6 +1466,7 @@
     )
     bias = dot(jnp.ones((8, n * own), low), ends, ((1,), (1,)))
     now[0, 7:8, 0 : bias.shape[1]] = bias[0:1]
+    gathered()
     project.first()
     for item in feeds:
         item.spread3()
@@ -1529,6 +1536,7 @@
     stage_end(1)
     project.everywhere()
     project.reduced()
+    attend.reduced()
 
     @pl.when(ctx < heads)
     def _():
@@ -1551,7 +1559,7 @@
     count = len(pieces)
     f32, low = jnp.float32, jnp.bfloat16
     whole = lambda item: jax.ShapeDtypeStruct((16,) + item.shape[1:], item.dtype)
-    wide, deep = attend_pieces.shape[2:]
+    wide, deep = attend_pieces.shape[1] // 4, attend_pieces.shape[2] // 2
     unit = (3, heads * HEAD_DIM, cols)
     result = pl.pallas_call(
         functools.partial(last_kernel, n, nc, heads, shared, count),
@@ -1578,7 +1586,7 @@
             DMA((2, nc)),
             DMA((2, nc)),
             DMA,
-            DMA((9,)),
+            DMA((10,)),
             pltpu.VMEM((n, own, cols), low),
             pltpu.VMEM((own, cols), f32),
             pltpu.VMEM((own, cols), f32),
@@ -1587,11 +1595,13 @@
             pltpu.VMEM(vectors.shape, f32),
         ]
         + LineScatter.scratch(n, own, cols, low)
-        + LineScatter.scratch(n, own // 2, cols, low) * 2
+        + LineScatter.scratch(n, own // 4, cols, low) * 4
         + StripSum.reduce_scratch(unit, low)
         + PlaneSum.spread_scratch()
         + [item for _ in pieces for item in PlaneSum.spread_scratch()]
         + [pltpu.VMEM((n, wide, deep), low), DMA((n,)), DMA((n,)), DMA, pltpu.VMEM((wide, deep), low)]
+        + [pltpu.VMEM(attend_pieces.shape, low), pltpu.VMEM((2, 2, wide, deep), low)]
+        + StripSum.reduce_scratch(attend_pieces.shape, low)
         + [DMA((8,)), DMA((8,)), DMA, pltpu.VMEM((2,) + vectors.shape, f32)]
         + [pltpu.VMEM((size,) + vectors.shape, f32) for size in (n, 2 * nc)]
         + [DMA((size,)) for size in (n, 2 * nc) for _ in range(2)],

time: 218 us -> 217 us (level)
  local copies, waits for them, and re-layouts: 8.34 us -> 11.4 us
    pallas_call x1, Pallas kernels: 54.2 us -> 63.1 us  [last_part(): pl.pallas_call(functools.partial(last_kernel, n, nc, heads, shared, count...]
    pallas_call x1, Pallas kernels: 81 us -> 75.9 us  [feed_part(): pl.pallas_call(functools.partial(feed_kernel, n, nc, heads, chunks), out_...]
    pallas_call x1, Pallas kernels: 16 us -> 12.8 us  [attend_backward(): pl.pallas_call(functools.partial(backward_kernel, half, heads), out_shape...]
    pallas_call x1, Pallas kernels: 13.2 us -> 10.7 us  [attend_forward(): pl.pallas_call(functools.partial(forward_kernel, half, heads), out_shape=...]
    unnamed x38 -> x48, local copies, waits for them, and re-layouts: 5.3 us -> 7.33 us
where the time goes in v3:
time: 217 us; the launch traced here: 219 us
  Pallas kernels  202 us (93%)
  local copies, waits for them, and re-layouts  11.4 us (5%)
  other arithmetic  4.97 us (2%)
    pallas_call x1, Pallas kernels, feed_part(): pl.pallas_call(functools.partial(feed_kernel, n, nc, heads, chunks), out_...  75.9 us
    pallas_call x1, Pallas kernels, last_part(): pl.pallas_call(functools.partial(last_kernel, n, nc, heads, shared, count...  63.1 us
    pallas_call x1, Pallas kernels, start_part(): pl.pallas_call(functools.partial(start_kernel, n, nc, heads), out_shape=(...  39.4 us
    pallas_call x1, Pallas kernels, attend_backward(): pl.pallas_call(functools.partial(backward_kernel, half, heads), out_shape...  12.8 us
    pallas_call x1, Pallas kernels, attend_forward(): pl.pallas_call(functools.partial(forward_kernel, half, heads), out_shape=...  10.7 us
    unnamed x48, local copies, waits for them, and re-layouts  7.33 us
    convert_element_type x3, other arithmetic, per_device(): f32 = lambda value: value.astype(jnp.float32)  4.9 us

profile of v3, /device:TPU:0, one launch (start us, length us, event | category | flops | bytes accessed | tf_op | source)
XLA Modules:
  0.0 219.1 jit_solution(5133524407163688158)
XLA Ops:
  0.6 0.1 pad.1.clone
  0.7 0.8 fusion
  1.5 0.1 maximum_bitcast_fusion
  1.6 0.0 copy-start.14
  1.6 0.0 copy-start.22
  1.6 0.9 copy.30.b_hbm
  2.5 0.0 copy-start.3
  2.5 0.0 copy-start.5
  2.5 0.0 copy-start.6
  2.5 0.0 copy-start.18
  2.5 0.0 copy-start.19
  2.5 0.0 copy-start.20
  2.5 0.0 copy-start.21
  2.5 39.4 %shard_map.263 = (bf16[4,192,768]{2,1,0:T(8,128)(2,1)}, bf16[4,192,768]{2,1,0:T(8,128)(2,1)}, bf16[4,3,64,768]{3,2,1,0:T(8,128)(2,1)}, bf16[4,192,768]{2,1,0:T(8,128)(2,1)}) custom-call(bf16[192,768]{1,0:T(8,128)(2,1)} %bitcast.21, f32[768]{0:T(1024)} %rest_3_.3, f32[768]{0:T(1024)} %shift_hbm.1, bf16[192,768]{1,0:T(8,128)(2,1)} %full_ref.1, ...), custom_call_target="tpu_custom_call" | custom-call | tf_op jit(solution)/shard_map/pallas_call | solution.py:1830
  41.9 0.0 copy-done.14
  41.9 0.0 copy-done.22
  41.9 0.0 copy-start
  41.9 1.3 copy-done
  43.1 0.0 copy-start.7
  43.2 10.7 %shard_map.264 = (bf16[16,64,192]{2,1,0:T(8,128)(2,1)S(1)}, f32[8,64,384]{2,1,0:T(8,128)S(1)}, f32[8,1,384]{2,1,0:T(1,128)S(1)}, s32[1,3072]{1,0:T(1,128)S(1)}) custom-call(s32[1,3072]{1,0:T(1,128)S(1)} %copy-done.14, s32[8]{0:T(128)S(1)} %copy-done.22, s32[1,3072]{1,0:T(1,128)S(1)} %copy-done.14, bf16[4,3,64,768]{3,2,1,0:T(8,128)(2,1)S(1)} %copy-done), custom_call_target="tpu_custom_call" | custom-call | tf_op jit(solution)/shard_map/pallas_call | solution.py:1948
  53.8 0.0 copy-done.3
  53.8 0.0 copy-done.5
  53.8 0.0 copy-done.6
  53.9 0.0 copy-done.18
  53.9 0.0 copy-done.19
  53.9 0.0 copy-done.20
  53.9 0.0 copy-done.21
  53.9 0.0 copy-done.7
  53.9 0.0 copy-start.8
  53.9 1.3 copy-done.8
  55.2 0.0 copy-start.9
  55.2 1.3 copy-done.9
  56.5 0.0 copy-start.1
  56.5 75.9 %shard_map.265 = (bf16[768,768]{1,0:T(8,128)(2,1)S(1)}, bf16[2,48,768]{2,1,0:T(8,128)(2,1)S(1)}, bf16[2,48,768]{2,1,0:T(8,128)(2,1)S(1)}, f32[192,768]{1,0:T(8,1...) custom-call(bf16[16,64,192]{2,1,0:T(8,128)(2,1)S(1)} %get-tuple-elem, ...), custom_call_target="tpu_custom_call" | custom-call | tf_op jit(solution)/shard_map/pallas_call | solution.py:1207
  132.3 0.0 copy-done.1
  132.3 0.0 copy-start.2
  132.3 0.0 copy-start.4
  132.4 0.0 copy-start.16
  132.4 0.0 copy-start.17
  132.4 12.8 %shard_map.266.x_ref = bf16[4,3,64,768]{3,2,1,0:T(8,128)(2,1)S(1)} custom-call(s32[1,3072]{1,0:T(1,128)S(1)} %copy-done.14, s32[8]{0:T(128)S(1)} %copy-done.22, s32[1,3072]{1,0:T(1,128)S(1)} %get-tuple-element.38.start_ref, bf16[4,3,64,768]{3,2,1,0:T(8,128)(2,1)S(1)} %copy-done.1, f32[8,64,384]{2,1,0:T(8,128)S(1)} %get-tuple-element.39.full_ref, ...), custom_call_target="tpu_custom_call" | custom-call | tf_op jit(solution)/shard_map/pallas_call | solution.py:2020
  145.2 0.0 copy-done.2
  145.2 0.0 copy-done.4
  145.2 0.0 copy-done.16
  145.2 0.0 copy-done.17
  145.2 63.1 %shard_map.267 = (bf16[192,768]{1,0:T(8,128)(2,1)S(1)}, bf16[192,768]{1,0:T(8,128)(2,1)S(1)}, f32[8,768]{1,0:T(8,128)S(1)}, bf16[3,192,768]{2,1,0:T(8,128)(2,1)S...) custom-call(bf16[4,3,64,768]{3,2,1,0:T(8,128)(2,1)S(1)} %shard_map.266.x_ref, ...), custom_call_target="tpu_custom_call" | custom-call | tf_op jit(solution)/shard_map/pallas_call | solution.py:1564
  208.4 0.0 copy-start.10
  208.4 0.7 copy-done.10
  209.1 0.0 copy-start.12
  209.1 0.7 copy-done.12
  209.8 0.0 copy-start.15
  209.8 0.6 copy-done.15
  210.4 0.1 slice.45
  210.5 0.6 slice.53
  211.1 1.7 slice_reduce_fusion
  212.7 0.9 convert_element_type.23
  213.6 1.3 convert_bitcast_fusion
  214.9 0.0 copy-start.13
  214.9 0.0 copy-start.11
  214.9 2.7 %bitcast_convert_fusion = (f32[768,768]{1,0:T(8,128)}, f32[768,768]{1,0:T(8,128)}) fusion(bf16[16,48,768]{2,1,0:T(8,128)(2,1)S(1)} %get-tuple-element.59, bf16[16,48,768]{2,1,0:T(8,128)(2,1)S(1)} %get-tuple-element.58), kind=kLoop, calls=%fused_computation.1 | loop fusion | flops 1179648 | bytes 7077888 | tf_op jit(solution)/shard_map/convert_element_type | solution.py:2095
  217.6 0.0 copy-done.13
  217.6 0.7 copy.33
  218.4 0.0 copy-done.11
  218.4 0.7 copy.34
  (1 shorter events, 0.0 us)
Async XLA Ops:
  1.6 40.3 %copy-start.14 = (s32[1,3072]{1,0:T(1,128)S(1)}, s32[1,3072]{1,0:T(1,128)}, u32[]{:S(2)}) copy-start(s32[1,3072]{1,0:T(1,128)} %seg_s.3) | copy-start | bytes 36868
  1.6 40.3 %copy-start.22 = (s32[8]{0:T(128)S(1)}, s32[8]{0:T(128)}, u32[]{:S(2)}) copy-start(s32[8]{0:T(128)} %order_ref.3) | copy-start | bytes 100
  2.5 51.4 %copy-start.3 = (bf16[1,192,768]{2,1,0:T(8,128)(2,1)S(1)}, bf16[1,192,768]{2,1,0:T(8,128)(2,1)}, u32[]{:S(2)}) copy-start(bf16[1,192,768]{2,1,0:T(8,128)(2,1)} %param.16) | copy-start | bytes 884740
  2.5 51.4 %copy-start.5 = (bf16[1,192,768]{2,1,0:T(8,128)(2,1)S(1)}, bf16[1,192,768]{2,1,0:T(8,128)(2,1)}, u32[]{:S(2)}) copy-start(bf16[1,192,768]{2,1,0:T(8,128)(2,1)} %param.31) | copy-start | bytes 884740
  2.5 51.4 %copy-start.6 = (bf16[768,768]{1,0:T(8,128)(2,1)S(1)}, bf16[768,768]{1,0:T(8,128)(2,1)}, u32[]{:S(2)}) copy-start(bf16[768,768]{1,0:T(8,128)(2,1)} %rest_5_.1) | copy-start | bytes 3538948
  2.5 51.4 %copy-start.18 = (f32[768]{0:T(1024)S(1)}, f32[768]{0:T(1024)}, u32[]{:S(2)}) copy-start(f32[768]{0:T(1024)} %rest_2_.1) | copy-start | bytes 9220
  2.5 51.4 %copy-start.19 = (f32[768]{0:T(1024)S(1)}, f32[768]{0:T(1024)}, u32[]{:S(2)}) copy-start(f32[768]{0:T(1024)} %rest_3_.2) | copy-start | bytes 9220
  2.5 51.4 %copy-start.20 = (f32[768]{0:T(1024)S(1)}, f32[768]{0:T(1024)}, u32[]{:S(2)}) copy-start(f32[768]{0:T(1024)} %rest_4_.1) | copy-start | bytes 9220
  2.5 51.4 %copy-start.21 = (f32[768]{0:T(1024)S(1)}, f32[768]{0:T(1024)}, u32[]{:S(2)}) copy-start(f32[768]{0:T(1024)} %rest_7_.1) | copy-start | bytes 9220
  41.9 1.3 copy-start
  43.1 10.8 %copy-start.7 = (bf16[768,768]{1,0:T(8,128)(2,1)S(1)}, bf16[768,768]{1,0:T(8,128)(2,1)}, u32[]{:S(2)}) copy-start(bf16[768,768]{1,0:T(8,128)(2,1)} %rest_6_.1) | copy-start | bytes 3538948
  53.9 1.3 copy-start.8
  55.2 1.3 copy-start.9
  56.5 75.9 %copy-start.1 = (bf16[4,3,64,768]{3,2,1,0:T(8,128)(2,1)S(1)}, bf16[4,3,64,768]{3,2,1,0:T(8,128)(2,1)}, u32[]{:S(2)}) copy-start(bf16[4,3,64,768]{3,2,1,0:T(8,128)(2,1)} %get-tuple-element.37.qkv_ref) | copy-start | bytes 3538948
  132.3 12.8 %copy-start.2 = (bf16[3,768,192]{1,2,0:T(8,128)(2,1)S(1)}, bf16[3,768,192]{1,2,0:T(8,128)(2,1)}, u32[]{:S(2)}) copy-start(bf16[3,768,192]{1,2,0:T(8,128)(2,1)} %param.19) | copy-start | bytes 2654212
  132.3 12.8 %copy-start.4 = (bf16[4,192,768]{2,1,0:T(8,128)(2,1)S(1)}, bf16[4,192,768]{2,1,0:T(8,128)(2,1)}, u32[]{:S(2)}) copy-start(bf16[4,192,768]{2,1,0:T(8,128)(2,1)} %get-tuple-element.45) | copy-start | bytes 3538948
  132.4 12.8 %copy-start.16 = (f32[768]{0:T(1024)S(1)}, f32[768]{0:T(1024)}, u32[]{:S(2)}) copy-start(f32[768]{0:T(1024)} %rest_3_.3) | copy-start | bytes 9220
  132.4 12.8 %copy-start.17 = (f32[768]{0:T(1024)S(1)}, f32[768]{0:T(1024)}, u32[]{:S(2)}) copy-start(f32[768]{0:T(1024)} %bias_hbm.1) | copy-start | bytes 9220
  208.4 0.7 copy-start.10
  209.1 0.7 copy-start.12
  209.8 0.6 copy-start.15
  214.9 2.7 %copy-start.13 = (bf16[192,768]{1,0:T(8,128)(2,1)S(1)}, bf16[192,768]{1,0:T(8,128)(2,1)}, u32[]{:S(2)}) copy-start(bf16[192,768]{1,0:T(8,128)(2,1)} %copy-done.12) | copy-start | bytes 884740
  214.9 3.4 %copy-start.11 = (bf16[192,768]{1,0:T(8,128)(2,1)S(1)}, bf16[192,768]{1,0:T(8,128)(2,1)}, u32[]{:S(2)}) copy-start(bf16[192,768]{1,0:T(8,128)(2,1)} %copy-done.10) | copy-start | bytes 884740

commit v4 on v2

--- a/solution.py
+++ b/solution.py
@@ -999,7 +999,7 @@
 
         if s == n - 3:
             break
-    columns = 256
+    columns = wide
 
     def work(block):
         here = rows_of(block)
@@ -1205,7 +1205,7 @@
 def feed_part(pieces, tokens, out_weight, vectors, up, down, bias, near, cotangent, n, nc, heads, collective_id):
     rows, width = tokens.shape
     wide = up.shape[1]
-    chunks = 2
+    chunks = 4
     total = n * rows
     low, f32 = jnp.bfloat16, jnp.float32
     unit = (16, wide // 16, width)
@@ -1841,7 +1841,7 @@
         ]
         + [DMA((2, n - 1)) for _ in range(6)]
         + [DMA((4,)), DMA((4,)), DMA((2, nc)), DMA((2, nc)), DMA((6,))],
-        compiler_params=remote_params(collective_id, 56),
+        compiler_params=remote_params(collective_id, 44),
     )(tokens, gain, shift, w, project_weight, bias, cotangent)
     return full.reshape(n * rows, cols), weight.reshape(n * wide, deep), qkv, grads
 

time: 218 us -> 214 us (0.982)
  Pallas kernels: 204 us -> 199 us
    pallas_call x1, Pallas kernels: 81 us -> 77.9 us  [feed_part(): pl.pallas_call(functools.partial(feed_kernel, n, nc, heads, chunks), out_...]
    pallas_call x1, Pallas kernels: 39.3 us -> 37.2 us  [start_part(): pl.pallas_call(functools.partial(start_kernel, n, nc, heads), out_shape=(...]
    unnamed x38 -> x40, local copies, waits for them, and re-layouts: 5.3 us -> 6.91 us
where the time goes in v4:
time: 214 us
  Pallas kernels  199 us (93%)
  local copies, waits for them, and re-layouts  9.24 us (4%)
  other arithmetic  4.97 us (2%)
    pallas_call x1, Pallas kernels, feed_part(): pl.pallas_call(functools.partial(feed_kernel, n, nc, heads, chunks), out_...  77.9 us
    pallas_call x1, Pallas kernels, last_part(): pl.pallas_call(functools.partial(last_kernel, n, nc, heads, shared, count...  56.3 us
    pallas_call x1, Pallas kernels, start_part(): pl.pallas_call(functools.partial(start_kernel, n, nc, heads), out_shape=(...  37.2 us
    pallas_call x1, Pallas kernels, attend_backward(): pl.pallas_call(functools.partial(backward_kernel, half, heads), out_shape...  14.9 us
    pallas_call x1, Pallas kernels, attend_forward(): pl.pallas_call(functools.partial(forward_kernel, half, heads), out_shape=...  12.2 us
    unnamed x40, local copies, waits for them, and re-layouts  6.91 us
    convert_element_type x3, other arithmetic, per_device(): f32 = lambda value: value.astype(jnp.float32)  4.9 us

profile of v4, /device:TPU:0, one launch (start us, length us, event | category | flops | bytes accessed | tf_op | source)
XLA Modules:
  0.0 213.6 jit_solution(4337936801596946439)
XLA Ops:
  0.6 0.8 fusion
  1.4 0.1 pad.1.clone
  1.5 0.1 maximum_bitcast_fusion
  1.6 0.0 copy-start.9
  1.6 0.0 copy-start.18
  1.6 0.2 copy.30.b_hbm
  1.7 0.0 copy-start
  1.7 1.2 copy-done
  2.9 0.0 copy-start.2
  2.9 1.0 copy-done.2
  3.9 0.0 copy-start.4
  3.9 1.0 copy-done.4
  4.8 0.0 copy-start.8
  4.8 1.0 copy-done.8
  5.8 0.0 copy-start.10
  5.8 0.7 copy-done.10
  6.5 0.0 copy-start.12
  6.5 0.7 copy-done.12
  7.2 0.0 copy-start.3
  7.2 0.0 copy-start.5
  7.2 0.0 copy-start.6
  7.2 0.0 copy-start.7
  7.2 0.0 copy-start.14
  7.2 0.0 copy-start.15
  7.2 0.0 copy-start.16
  7.2 0.0 copy-start.17
  7.2 37.2 %shard_map.263 = (bf16[4,192,768]{2,1,0:T(8,128)(2,1)S(1)}, bf16[4,192,768]{2,1,0:T(8,128)(2,1)S(1)}, bf16[4,3,64,768]{3,2,1,0:T(8,128)(2,1)S(1)}, bf16[4,192,768]{2,1,0:T(8,128)(2,1)S(1)}) custom-call(bf16[192,768]{1,0:T(8,128)(2,1)S(1)} %bitcast.21, f32[768]{0:T(1024)S(1)} %copy-done.10, f32[768]{0:T(1024)S(1)} %copy-done.12, ...), custom_call_target="tpu_custom_call" | custom-call | tf_op jit(solution)/shard_map/pallas_call | solution.py:1820
  44.4 0.0 copy-done.9
  44.4 0.0 copy-done.18
  44.4 12.2 %shard_map.264 = (bf16[16,64,192]{2,1,0:T(8,128)(2,1)S(1)}, f32[8,64,384]{2,1,0:T(8,128)S(1)}, f32[8,1,384]{2,1,0:T(1,128)S(1)}, s32[1,3072]{1,0:T(1,128)S(1)}) custom-call(s32[1,3072]{1,0:T(1,128)S(1)} %copy-done.9, s32[8]{0:T(128)S(1)} %copy-done.18, s32[1,3072]{1,0:T(1,128)S(1)} %copy-done.9, bf16[4,3,64,768]{3,2,1,0:T(8,128)(2,1)S(1)} %get-tuple-element.37.qkv_ref), custom_call_target="tpu_custom_call" | custom-call | tf_op jit(solution)/shard_map/pallas_call | solution.py:1938
  56.7 0.0 copy-done.3
  56.7 0.0 copy-done.5
  56.7 0.0 copy-done.6
  56.7 0.0 copy-done.7
  56.7 0.0 copy-done.14
  56.7 0.0 copy-done.15
  56.7 0.0 copy-done.16
  56.7 0.0 copy-done.17
  56.7 77.9 %shard_map.265 = (bf16[768,768]{1,0:T(8,128)(2,1)S(1)}, bf16[2,48,768]{2,1,0:T(8,128)(2,1)S(1)}, bf16[2,48,768]{2,1,0:T(8,128)(2,1)S(1)}, f32[192,768]{1,0:T(8,1...) custom-call(bf16[16,64,192]{2,1,0:T(8,128)(2,1)S(1)} %get-tuple-elem, ...), custom_call_target="tpu_custom_call" | custom-call | tf_op jit(solution)/shard_map/pallas_call | solution.py:1213
  134.6 0.0 copy-start.1
  134.7 0.0 copy-start.11
  134.7 0.0 copy-start.13
  134.7 14.9 %shard_map.266.x_ref = bf16[4,3,64,768]{3,2,1,0:T(8,128)(2,1)S(1)} custom-call(s32[1,3072]{1,0:T(1,128)S(1)} %copy-done.9, s32[8]{0:T(128)S(1)} %copy-done.18, s32[1,3072]{1,0:T(1,128)S(1)} %get-tuple-element.38.start_ref, bf16[4,3,64,768]{3,2,1,0:T(8,128)(2,1)S(1)} %get-tuple-element.37.qkv_ref, f32[8,64,384]{2,1,0:T(8,128)S(1)} %get-tuple-element.39.full_ref, ...), custom_call_target="tpu_custom_call" | custom-call | tf_op jit(solution)/shard_map/pallas_call | solution.py:2010
  149.6 0.0 copy-done.1
  149.6 0.0 copy-done.11
  149.6 0.0 copy-done.13
  149.6 56.3 %shard_map.267 = (bf16[192,768]{1,0:T(8,128)(2,1)S(1)}, bf16[192,768]{1,0:T(8,128)(2,1)S(1)}, f32[8,768]{1,0:T(8,128)S(1)}, bf16[3,192,768]{2,1,0:T(8,128)(2,1)S...) custom-call(bf16[4,3,64,768]{3,2,1,0:T(8,128)(2,1)S(1)} %shard_map.266.x_ref, ...), custom_call_target="tpu_custom_call" | custom-call | tf_op jit(solution)/shard_map/pallas_call | solution.py:1556
  206.0 2.7 %bitcast_convert_fusion = (f32[768,768]{1,0:T(8,128)}, f32[768,768]{1,0:T(8,128)}) fusion(bf16[16,48,768]{2,1,0:T(8,128)(2,1)S(1)} %get-tuple-element.59, bf16[16,48,768]{2,1,0:T(8,128)(2,1)S(1)} %get-tuple-element.58), kind=kLoop, calls=%fused_computation.1 | loop fusion | flops 1179648 | bytes 7077888 | tf_op jit(solution)/shard_map/convert_element_type | solution.py:2085
  208.7 1.3 convert_bitcast_fusion
  210.0 0.9 convert_element_type.23
  210.9 0.7 slice_reduce_fusion
  211.5 0.1 slice.45
  211.6 0.6 slice.53
  212.2 0.7 copy.33
  212.9 0.7 copy.34
  (1 shorter events, 0.0 us)
Async XLA Ops:
  1.6 42.8 %copy-start.9 = (s32[1,3072]{1,0:T(1,128)S(1)}, s32[1,3072]{1,0:T(1,128)}, u32[]{:S(2)}) copy-start(s32[1,3072]{1,0:T(1,128)} %seg_s.3) | copy-start | bytes 36868
  1.6 42.8 %copy-start.18 = (s32[8]{0:T(128)S(1)}, s32[8]{0:T(128)}, u32[]{:S(2)}) copy-start(s32[8]{0:T(128)} %order_ref.3) | copy-start | bytes 100
  1.7 1.2 copy-start
  2.9 1.0 copy-start.2
  3.9 1.0 copy-start.4
  4.8 1.0 copy-start.8
  5.8 0.7 copy-start.10
  6.5 0.7 copy-start.12
  7.2 49.5 %copy-start.3 = (bf16[1,192,768]{2,1,0:T(8,128)(2,1)S(1)}, bf16[1,192,768]{2,1,0:T(8,128)(2,1)}, u32[]{:S(2)}) copy-start(bf16[1,192,768]{2,1,0:T(8,128)(2,1)} %param.16) | copy-start | bytes 884740
  7.2 49.5 %copy-start.5 = (bf16[1,192,768]{2,1,0:T(8,128)(2,1)S(1)}, bf16[1,192,768]{2,1,0:T(8,128)(2,1)}, u32[]{:S(2)}) copy-start(bf16[1,192,768]{2,1,0:T(8,128)(2,1)} %param.31) | copy-start | bytes 884740
  7.2 49.5 %copy-start.6 = (bf16[768,768]{1,0:T(8,128)(2,1)S(1)}, bf16[768,768]{1,0:T(8,128)(2,1)}, u32[]{:S(2)}) copy-start(bf16[768,768]{1,0:T(8,128)(2,1)} %rest_5_.1) | copy-start | bytes 3538948
  7.2 49.5 %copy-start.7 = (bf16[768,768]{1,0:T(8,128)(2,1)S(1)}, bf16[768,768]{1,0:T(8,128)(2,1)}, u32[]{:S(2)}) copy-start(bf16[768,768]{1,0:T(8,128)(2,1)} %rest_6_.1) | copy-start | bytes 3538948
  7.2 49.5 %copy-start.14 = (f32[768]{0:T(1024)S(1)}, f32[768]{0:T(1024)}, u32[]{:S(2)}) copy-start(f32[768]{0:T(1024)} %rest_2_.1) | copy-start | bytes 9220
  7.2 49.5 %copy-start.15 = (f32[768]{0:T(1024)S(1)}, f32[768]{0:T(1024)}, u32[]{:S(2)}) copy-start(f32[768]{0:T(1024)} %rest_3_.2) | copy-start | bytes 9220
  7.2 49.5 %copy-start.16 = (f32[768]{0:T(1024)S(1)}, f32[768]{0:T(1024)}, u32[]{:S(2)}) copy-start(f32[768]{0:T(1024)} %rest_4_.1) | copy-start | bytes 9220
  7.2 49.5 %copy-start.17 = (f32[768]{0:T(1024)S(1)}, f32[768]{0:T(1024)}, u32[]{:S(2)}) copy-start(f32[768]{0:T(1024)} %rest_7_.1) | copy-start | bytes 9220
  134.6 15.0 %copy-start.1 = (bf16[3,768,192]{1,2,0:T(8,128)(2,1)S(1)}, bf16[3,768,192]{1,2,0:T(8,128)(2,1)}, u32[]{:S(2)}) copy-start(bf16[3,768,192]{1,2,0:T(8,128)(2,1)} %param.19) | copy-start | bytes 2654212
  134.7 15.0 %copy-start.11 = (f32[768]{0:T(1024)S(1)}, f32[768]{0:T(1024)}, u32[]{:S(2)}) copy-start(f32[768]{0:T(1024)} %rest_3_.3) | copy-start | bytes 9220
  134.7 15.0 %copy-start.13 = (f32[768]{0:T(1024)S(1)}, f32[768]{0:T(1024)}, u32[]{:S(2)}) copy-start(f32[768]{0:T(1024)} %bias_hbm.1) | copy-start | bytes 9220
